TPU v7x, 32 devices: a whole 2x2x4 slice. The times are simulated.
32 devices in a mesh: heads: 8 (over y, x, core), batch: 4 (over z).
Axes of the slice: x: 2, y: 2, z: 4, core: 2. Of those that a mesh axis runs over, the one named last changes fastest.
Arguments:
- tokens: bfloat16 [2, 4, 1024, 2048], P(None, 'batch', 'heads'), may hold values from -6 to 6
- cotangent: bfloat16 [2, 4, 1024, 2048], P(None, 'batch', 'heads'), may hold values from -6 to 6
- doc_lengths: int32 [2, 4, 4], P(None, 'batch'), may hold values from 1 to 768, 1024 in all within a row
- pad_mask: int32 [2, 4, 1024], P(None, 'batch'), may hold values 0 or 1
- w_query: bfloat16 [2048, 1024], P(None, 'heads'), may hold values from -0.1875 to 0.1875
- w_key: bfloat16 [2048, 1024], P(None, 'heads'), may hold values from -0.1875 to 0.1875
- w_value: bfloat16 [2048, 1024], P(None, 'heads'), may hold values from -0.125 to 0.125
- w_out: bfloat16 [1024, 2048], P('heads'), may hold values from -0.75 to 0.75
- w_gate: bfloat16 [2048, 8192], P(None, 'heads'), may hold values from -0.125 to 0.125
- w_up: bfloat16 [2048, 8192], P(None, 'heads'), may hold values from -0.125 to 0.125
- w_down: bfloat16 [8192, 2048], P('heads'), may hold values from -0.0625 to 0.0625
- norm_attn: float32 [2048], replicated, may hold values from 0.1 to 1.9
- norm_mlp: float32 [2048], replicated, may hold values from 0.1 to 1.9
- mix_gate: float32 [8], P('heads'), may hold values from -2 to 2
Outputs:
- layer_out: bfloat16 [2, 4, 1024, 2048], P(None, 'batch', 'heads')
- grad_tokens: float32 [2, 4, 1024, 2048], P(None, 'batch', 'heads')
- grad_w_query: float32 [2048, 1024], P(None, 'heads')
- grad_w_key: float32 [2048, 1024], P(None, 'heads')
- grad_w_value: float32 [2048, 1024], P(None, 'heads')
- grad_w_out: float32 [1024, 2048], P('heads')
- grad_w_gate: float32 [2048, 8192], P(None, 'heads')
- grad_w_up: float32 [2048, 8192], P(None, 'heads')
- grad_w_down: float32 [8192, 2048], P('heads')
- grad_norm_attn: float32 [2048], replicated
- grad_norm_mlp: float32 [2048], replicated
- grad_mix_gate: float32 [8], P('heads')
Inputs may be any that keep to these rules, and one draw needn't show every extreme that they name: `doc_lengths`: the 4 lengths of a sequence sum to 1024; the longest is 768.
All inputs are finite; a program needn't handle non-finite values. No bound on the sum of `pad_mask` on one device may be relied on, other than what follows from the above.
Results may differ from a plain program's by a relative error of at most 0.018.
Values may be sent and summed in bfloat16 or wider, within the bound.
No kernel may reach another device: no remote copies, remote signals or barrier semaphores. Data moves between devices by JAX's collectives and lax.ppermute only.
A program may use at most 256 MiB of HBM per device.

v0:
```python
import jax
import jax.numpy as jnp
from jax import lax
from jax.sharding import PartitionSpec as P

DH = 128
SEG = 512
SEGS = 2
LEN = 1024
MICRO = 2
epsilon = 1e-05
big_negative = -1e30


def dot_rows(left_mat, right_mat):
    return lax.dot_general(
        left_mat, right_mat, (((1,), (1,)), ((), ())), preferred_element_type=jnp.float32
    )


def dot_cols(left_mat, right_mat):
    return lax.dot_general(
        left_mat, right_mat, (((0,), (0,)), ((), ())), preferred_element_type=jnp.float32
    )


def batch_mm(left, right):
    return lax.dot_general(
        left, right, (((2,), (1,)), ((0,), (0,))), preferred_element_type=jnp.float32
    )


def batch_mt(left, right):
    return lax.dot_general(
        left, right, (((2,), (2,)), ((0,), (0,))), preferred_element_type=jnp.float32
    )


def batch_tm(left, right):
    return lax.dot_general(
        left, right, (((1,), (1,)), ((0,), (0,))), preferred_element_type=jnp.float32
    )


def norm_scale(row_block):
    return lax.rsqrt(jnp.mean(row_block * row_block, axis=-1, keepdims=True) + epsilon)


def norm_back(row_block, row_scale, gain_vec, upstream):
    shaped = upstream * gain_vec
    inner = jnp.mean(shaped * row_block, axis=-1, keepdims=True)
    d_rows = row_scale * shaped - row_block * row_scale * row_scale * row_scale * inner
    d_gain = jnp.sum(upstream * row_block * row_scale, axis=0)
    return (d_rows, d_gain)


def positive(values_in):
    return jnp.where(values_in > 0, values_in + 1.0, jnp.exp(values_in))


def local_mask(begin_row, positions, doc_ids, valid_keys):
    seg_pos = positions[begin_row : begin_row + SEG]
    seg_doc = doc_ids[:, begin_row : begin_row + SEG]
    seg_valid = valid_keys[:, begin_row : begin_row + SEG]
    same_doc = seg_doc[:, :, None] == seg_doc[:, None, :]
    causal = (seg_pos[None, :] <= seg_pos[:, None])[None]
    diagonal = (seg_pos[None, :] == seg_pos[:, None])[None]
    return same_doc & causal & (seg_valid[:, None, :] | diagonal)


def memory_mask(begin_row, doc_ids, valid_keys):
    seg_doc = doc_ids[:, begin_row : begin_row + SEG]
    return (seg_doc[:, :, None] == doc_ids[:, None, :begin_row]) & valid_keys[:, None, :begin_row]


def head_forward(query_all, key_all, value_all, share, positions, doc_ids, valid_keys):
    score_scale = DH ** (-0.5)
    pos_query = positive(query_all.astype(jnp.float32)).astype(jnp.bfloat16)
    pos_key = positive(key_all.astype(jnp.float32)).astype(jnp.bfloat16)
    kept = []
    dotted_parts, recalled_parts = ([], [])
    for segment in range(SEGS):
        rows = slice(segment * SEG, (segment + 1) * SEG)
        before = slice(0, segment * SEG)
        allowed = local_mask(segment * SEG, positions, doc_ids, valid_keys)
        scores = jnp.where(
            allowed, batch_mt(query_all[:, rows], key_all[:, rows]) * score_scale, big_negative
        )
        shifted = jnp.exp(scores - jnp.max(scores, axis=2, keepdims=True))
        soft_probs = shifted / jnp.sum(shifted, axis=2, keepdims=True)
        dotted_parts.append(batch_mm(soft_probs.astype(jnp.bfloat16), value_all[:, rows]))
        if segment == 0:
            recalled_parts.append(jnp.zeros((query_all.shape[0], SEG, DH), jnp.float32))
            kept.append((soft_probs,))
        else:
            mem_allowed = memory_mask(segment * SEG, doc_ids, valid_keys)
            weights = jnp.where(mem_allowed, batch_mt(pos_query[:, rows], pos_key[:, before]), 0.0)
            row_total = jnp.sum(weights, axis=2, keepdims=True)
            denominator = jnp.maximum(row_total, 1.0)
            weights_low = weights.astype(jnp.bfloat16)
            numerator = batch_mm(weights_low, value_all[:, before])
            recalled_parts.append(numerator / denominator)
            kept.append((soft_probs, mem_allowed, row_total, weights_low, numerator))
    dotted = jnp.concatenate(dotted_parts, axis=1)
    recalled = jnp.concatenate(recalled_parts, axis=1)
    mixed_head = share * recalled + (1.0 - share) * dotted
    return (mixed_head, dotted, recalled, pos_query, pos_key, kept)


def head_backward(query_all, key_all, value_all, share, d_mixed, forward_kept):
    _, dotted, recalled, pos_query, pos_key, kept = forward_kept
    score_scale = DH ** (-0.5)
    query_float = query_all.astype(jnp.float32)
    key_float = key_all.astype(jnp.float32)
    d_share = jnp.sum(d_mixed * (recalled - dotted)) * share * (1.0 - share)
    d_dotted = ((1.0 - share) * d_mixed).astype(jnp.bfloat16)
    d_recalled = share * d_mixed
    nothing = jnp.zeros((query_all.shape[0], SEG, DH), jnp.float32)
    d_query, d_key, d_value, d_posq, d_posk = [[nothing for _ in range(SEGS)] for _ in range(5)]
    for segment in range(SEGS):
        rows = slice(segment * SEG, (segment + 1) * SEG)
        before = slice(0, segment * SEG)
        soft_probs = kept[segment][0]
        d_dot_seg = d_dotted[:, rows]
        d_value[segment] += batch_tm(soft_probs.astype(jnp.bfloat16), d_dot_seg)
        d_probs = batch_mt(d_dot_seg, value_all[:, rows])
        d_scores = (
            soft_probs * (d_probs - jnp.sum(soft_probs * d_probs, axis=2, keepdims=True))
        ).astype(jnp.bfloat16)
        d_query[segment] += batch_mm(d_scores, key_all[:, rows]) * score_scale
        d_key[segment] += batch_tm(d_scores, query_all[:, rows]) * score_scale
        if segment > 0:
            _, mem_allowed, row_total, weights_low, numerator = kept[segment]
            denominator = jnp.maximum(row_total, 1.0)
            d_recall_seg = d_recalled[:, rows]
            d_numer = (d_recall_seg / denominator).astype(jnp.bfloat16)
            d_denom = jnp.where(
                row_total > 1.0,
                -jnp.sum(d_recall_seg * numerator, axis=2, keepdims=True)
                / (denominator * denominator),
                0.0,
            )
            d_weights = jnp.where(
                mem_allowed, batch_mt(d_numer, value_all[:, before]) + d_denom, 0.0
            ).astype(jnp.bfloat16)
            d_posq[segment] += batch_mm(d_weights, pos_key[:, before])
            d_posk_all = batch_tm(d_weights, pos_query[:, rows])
            d_value_all = batch_tm(weights_low, d_numer)
            for earlier in range(segment):
                part = slice(earlier * SEG, (earlier + 1) * SEG)
                d_posk[earlier] += d_posk_all[:, part]
                d_value[earlier] += d_value_all[:, part]
    d_query, d_key, d_value, d_posq, d_posk = [
        jnp.concatenate(parts, axis=1) for parts in (d_query, d_key, d_value, d_posq, d_posk)
    ]
    d_query = d_query + d_posq * jnp.where(query_float > 0, 1.0, jnp.exp(query_float))
    d_key = d_key + d_posk * jnp.where(key_float > 0, 1.0, jnp.exp(key_float))
    return (
        d_query.astype(jnp.bfloat16),
        d_key.astype(jnp.bfloat16),
        d_value.astype(jnp.bfloat16),
        d_share,
    )


class Chain:

    def __init__(self, axis, size, depth):
        self.axis, self.size, self.depth = (axis, size, depth)
        self.place = lax.axis_index(axis)
        half = size // 2
        self.stages = [("in", [(s - 1, s), (size - s, size - 1 - s)]) for s in range(1, half)]
        self.stages.append(("in", [(half - 1, half), (half, half - 1)]))
        self.stages += [
            ("out", [(s, s - 1), (size - 1 - s, size - s)]) for s in range(half - 1, 0, -1)
        ]
        self.entered = []
        self.last = [None] * len(self.stages)

    def add(self, array):
        if self.size == 1:
            return array
        if self.size % 2:
            return lax.psum(array, self.axis)
        if len(self.entered) >= self.depth:
            array, _ = lax.optimization_barrier((array, self.entered[-self.depth]))
        for number, (kind, pairs) in enumerate(self.stages):
            arrived = lax.ppermute(array, self.axis, pairs)
            if self.last[number] is not None:
                array, arrived, _ = lax.optimization_barrier((array, arrived, self.last[number]))
            if kind == "in":
                array = array + arrived
            else:
                receives = jnp.zeros((), jnp.bool_)
                for _, target in pairs:
                    receives = receives | (self.place == target)
                array = jnp.where(receives, arrived, array)
            self.last[number] = array
            if number == 0:
                self.entered.append(array)
        return array


def per_device(
    tokens,
    cotangent,
    doc_lengths,
    pad_mask,
    w_query,
    w_key,
    w_value,
    w_out,
    w_gate,
    w_up,
    w_down,
    norm_attn,
    norm_mlp,
    mix_gate,
    *,
    n_heads,
    n_batch
):
    width = tokens.shape[-1]
    rows = tokens.shape[2]
    own_rows = MICRO * rows
    all_rows = n_heads * own_rows
    hidden_cols = w_gate.shape[1]
    here = lax.axis_index("heads")
    low = jnp.bfloat16

    def by_sequence(array):
        cols = array.shape[-1]
        return (
            array.reshape(n_heads, MICRO, rows, cols)
            .transpose(1, 0, 2, 3)
            .reshape(MICRO, LEN, cols)
        )

    def by_device(array):
        cols = array.shape[-1]
        return (
            array.reshape(MICRO, n_heads, rows, cols).transpose(1, 0, 2, 3).reshape(all_rows, cols)
        )

    def gather(array):
        return lax.all_gather(array, "heads", axis=0, tiled=True)

    def scatter(array):
        return lax.psum_scatter(array, "heads", scatter_dimension=0, tiled=True)

    def own(array):
        return lax.dynamic_slice_in_dim(array, here * own_rows, own_rows, 0)

    w_qkv = jnp.concatenate([w_query, w_key, w_value], axis=1)
    w_gate_up = jnp.concatenate([w_gate, w_up], axis=1)
    share = jax.nn.sigmoid(mix_gate)[0]
    positions = jnp.arange(LEN, dtype=jnp.int32)
    doc_ends = jnp.cumsum(doc_lengths[:, 0], axis=1)
    doc_ids = jnp.sum((positions[None, :, None] >= doc_ends[:, None, :]).astype(jnp.int32), axis=2)
    valid_keys = pad_mask[:, 0] == 1
    tok_own = tokens.reshape(own_rows, width)
    cot_own = cotangent.reshape(own_rows, width)
    tok_all = gather(tok_own)
    w_out_all = gather(w_out)
    x_all = tok_all.astype(jnp.float32)
    h1_all = (x_all * norm_scale(x_all) * norm_attn).astype(low)
    qkv = jnp.dot(h1_all, w_qkv, preferred_element_type=jnp.float32).astype(low)
    query, key, value = [by_sequence(qkv[:, i * DH : (i + 1) * DH]) for i in range(3)]
    head_kept = head_forward(query, key, value, share, positions, doc_ids, valid_keys)
    mixed = by_device(head_kept[0].astype(low))
    mixed_all = lax.all_gather(mixed, "heads", axis=1, tiled=True)
    cot_all = gather(cot_own)
    y1_all = x_all + jnp.dot(mixed_all, w_out_all, preferred_element_type=jnp.float32)
    h2_all = (y1_all * norm_scale(y1_all) * norm_mlp).astype(low)
    x_own = tok_own.astype(jnp.float32)
    y1_own = own(y1_all)
    gate_up = jnp.dot(h2_all, w_gate_up, preferred_element_type=jnp.float32)
    gate_pre = gate_up[:, :hidden_cols]
    up_pre = gate_up[:, hidden_cols:]
    sig_gate = jax.nn.sigmoid(gate_pre)
    hidden = (gate_pre * sig_gate * up_pre).astype(low)
    d_hidden = dot_rows(cot_all, w_down)
    d_up = d_hidden * gate_pre * sig_gate
    d_gate = d_hidden * up_pre * sig_gate * (1.0 + gate_pre * (1.0 - sig_gate))
    d_gate_up = jnp.concatenate([d_gate, d_up], axis=1).astype(low)
    chain = Chain("batch", n_batch, 3)
    d_h2 = scatter(dot_rows(d_gate_up, w_gate_up).astype(low)).astype(jnp.float32)
    down_parts, gate_up_parts = ([], [])
    step = hidden_cols // 4
    for begin in range(0, hidden_cols, step):
        down_parts.append(chain.add(dot_cols(hidden[:, begin : begin + step], cot_all).astype(low)))
    step = width // 8
    for begin in range(0, width, step):
        gate_up_parts.append(
            chain.add(dot_cols(h2_all[:, begin : begin + step], d_gate_up).astype(low))
        )
    mlp_own = scatter(jnp.dot(hidden, w_down, preferred_element_type=jnp.float32).astype(low))
    layer_out = (y1_own + mlp_own.astype(jnp.float32)).astype(low)
    scale_mlp = norm_scale(y1_own)
    d_y1, gain_mlp_part = norm_back(y1_own, scale_mlp, norm_mlp, d_h2)
    d_y1 = d_y1 + cot_own.astype(jnp.float32)
    d_attn = d_y1.astype(low)
    d_mixed_own = dot_rows(d_attn, w_out_all).astype(low)
    d_mixed = lax.all_to_all(d_mixed_own, "heads", split_axis=1, concat_axis=0, tiled=True)
    grad_out = scatter(dot_cols(own(mixed_all), d_attn).astype(low))
    d_query, d_key, d_value, d_share = head_backward(
        query, key, value, share, by_sequence(d_mixed).astype(jnp.float32), head_kept
    )
    d_qkv = jnp.concatenate([by_device(d_query), by_device(d_key), by_device(d_value)], axis=1)
    d_h1 = scatter(dot_rows(d_qkv, w_qkv).astype(low)).astype(jnp.float32)
    grad_out = chain.add(grad_out)
    grad_qkv = chain.add(dot_cols(h1_all, d_qkv).astype(low))
    d_x, gain_attn_part = norm_back(x_own, norm_scale(x_own), norm_attn, d_h1)
    grad_tokens = (d_x + d_y1).reshape(tokens.shape)
    slots = jnp.where(jnp.arange(n_heads) == here, d_share, 0.0)
    sums = lax.psum(jnp.concatenate([gain_attn_part, gain_mlp_part, slots]), ("heads", "batch"))
    grad_mix = lax.dynamic_slice_in_dim(sums, 2 * width + here, 1, 0)
    wide = jnp.float32
    grad_qkv = grad_qkv.astype(wide)
    grad_gate_up = jnp.concatenate([p.astype(wide) for p in gate_up_parts], axis=0)
    grad_down = jnp.concatenate([p.astype(wide) for p in down_parts], axis=0)
    return (
        layer_out.reshape(tokens.shape),
        grad_tokens,
        grad_qkv[:, :DH],
        grad_qkv[:, DH : 2 * DH],
        grad_qkv[:, 2 * DH :],
        grad_out.astype(wide),
        grad_gate_up[:, :hidden_cols],
        grad_gate_up[:, hidden_cols:],
        grad_down,
        sums[:width],
        sums[width : 2 * width],
        grad_mix,
    )


def solution(mesh):
    in_specs = (
        P(None, "batch", "heads", None),
        P(None, "batch", "heads", None),
        P(None, "batch", None),
        P(None, "batch", None),
        P(None, "heads"),
        P(None, "heads"),
        P(None, "heads"),
        P("heads", None),
        P(None, "heads"),
        P(None, "heads"),
        P("heads", None),
        P(),
        P(),
        P("heads"),
    )
    out_specs = (
        P(None, "batch", "heads", None),
        P(None, "batch", "heads", None),
        P(None, "heads"),
        P(None, "heads"),
        P(None, "heads"),
        P("heads", None),
        P(None, "heads"),
        P(None, "heads"),
        P("heads", None),
        P(),
        P(),
        P("heads"),
    )

    def program(*arrays):
        return per_device(*arrays, n_heads=mesh.shape["heads"], n_batch=mesh.shape["batch"])

    return jax.shard_map(
        program, mesh=mesh, in_specs=in_specs, out_specs=out_specs, check_vma=False
    )
```

profile of v0, /device:TPU:0, one launch (start us, length us, event | category | flops | bytes accessed | tf_op | source)
XLA Modules:
  0.0 852.9 jit_solution(9633711189530872917)
XLA Ops:
  16.1 50.9 %all-gather.5.cloned.1.call-done = bf16[2048,2048]{1,0:T(8,128)(2,1)} async-done(((bf16[256,2048]{1,0:T(8,128)(2,1)}), bf16[2048,2048]{1,0:T(8,128)(2,1)}) %all-gather.5.cloned.1.call-update) | async-done | bytes 8388624 | tf_op jit(solution)/shard_map/all_gather | solution.py:246
  67.0 5.2 fusion.2
  72.8 4.8 convolution_convert_fusion.5
  87.3 2.9 fusion.56
  93.2 4.8 constant_dynamic-update-slice_fusion.4
  100.5 5.2 all-gather.9.cloned.1.call-done
  105.7 39.9 %all-gather.7.cloned.1.call-done = bf16[2048,1024]{1,0:T(8,128)(2,1)} async-done(((bf16[2048,128]{1,0:T(8,128)(2,1)}), bf16[2048,1024]{1,0:T(8,128)(2,1)}) %all-gather.7.cloned.1.call-update) | async-done | bytes 4194320 | tf_op jit(solution)/shard_map/all_gather | solution.py:271
  145.6 13.5 %multiply_reduce_fusion = (f32[2048]{0:T(1024)S(1)}, f32[2048,2048]{1,0:T(8,128)S(1)}) fusion(bf16[2048,1024]{1,0:T(8,128)(2,1)} %all-gather.7.cloned.1.call-done, bf16[1024,2048]{1,0:T(8,128)(2,1)} %all-gather.9.cloned.1.call-done, bf16[2048,2048]{1,0:T(8,128)(2,1)} %all-gather.5.cloned.1.call-done), kind=kOutput, calls=%fused_computation.9 | convolution fusion | flops 8606709760 | bytes 33562624 | tf_op jit(solution)/shard_map/dot_general | solution.py:273
  159.1 5.8 copy-done
  164.9 4.4 multiply_convert_fusion
  169.3 24.3 %fusion.125 = f32[2048,2048]{0,1:T(8,128)} fusion(bf16[2048,2048]{1,0:T(8,128)(2,1)} %multiply_convert_fusion, bf16[2048,2048]{1,0:T(8,128)(2,1)} %constant_dynamic-update-slice_fusion.3), kind=kOutput, calls=%fused_computation.223 | convolution fusion | flops 17179869184 | bytes 33554432 | tf_op jit(solution)/shard_map/dot_general | solution.py:277
  193.7 8.1 all-gather.11.cloned.1.call-done
  201.8 22.8 %multiply_convert_fusion.2 = (bf16[2048,1024]{0,1:T(8,128)(2,1)S(1)}, bf16[2048,1024]{0,1:T(8,128)(2,1)}, bf16[2048,1024]{0,1:T(8,128)(2,1)}) fusion(f32[2048,2048]{0,1:T(8,128)} %fusion.125, bf16[2048,2048]{1,0:T(8,128)(2,1)} %all-gather.11.cloned.1.call-done, bf16[1024,2048]{1,0:T(8,128)(2,1)} %param.24), kind=kOutput, calls=%fused_computation.12 | convolution fusion | flops 8623489024 | bytes 41943040 | tf_op jit(solution)/shard_map/dot_general | solution.py:16
  226.6 22.9 %convolution_convert_fusion.1 = bf16[2048,2048]{1,0:T(8,128)(2,1)} fusion(bf16[2048,2048]{1,0:T(8,128)(2,1)} %constant_dynamic-update-slice_fusion.3, bf16[2048,1024]{0,1:T(8,128)(2,1)} %get-tuple-element.249, bf16[2048,1024]{0,1:T(8,128)(2,1)S(1)} %get-tuple-element.248), kind=kOutput, calls=%fused_computation.16 | convolution fusion | flops 17200840704 | bytes 25165824 | tf_op jit(solution)/shard_map/dot_general | solution.py:16
  249.6 14.5 %convolution_convert_fusion.2 = bf16[2048,2048]{1,0:T(8,128)(2,1)} fusion(bf16[2048,1024]{0,1:T(8,128)(2,1)} %get-tuple-element.252, bf16[1024,2048]{1,0:T(8,128)(2,1)} %param.24), kind=kOutput, calls=%fused_computation.17 | convolution fusion | flops 8594128896 | bytes 16777216 | tf_op jit(solution)/shard_map/dot_general | solution.py:297
  266.3 6.2 convolution_convert_fusion.13
  272.6 3.9 collective-permute-start.1
  276.5 6.4 convolution_convert_fusion.14
  285.5 3.4 convolution_convert_fusion.15
  288.9 3.4 convolution_convert_fusion.9
  292.4 5.7 convolution_convert_fusion.10
  298.1 7.1 convolution_convert_fusion.16
  305.2 4.9 convolution_convert_fusion.11
  310.1 7.2 convolution_convert_fusion.7
  321.4 4.5 convolution_convert_fusion.12
  331.0 3.4 collective-permute-start.3
  336.7 3.1 fusion.16
  339.8 56.7 %reduce-scatter.5.cloned.1.call-done = bf16[256,2048]{1,0:T(8,128)(2,1)} async-done(((bf16[2048,2048]{1,0:T(8,128)(2,1)}), bf16[256,2048]{1,0:T(8,128)(2,1)}) %reduce-scatter.5.cloned.1.call-update) | async-done | bytes 1048592 | tf_op jit(solution)/shard_map/reduce_scatter | solution.py:249
  396.6 4.6 fusion.13
  403.4 4.2 all-to-all-start
  407.6 7.1 convolution_convert_fusion.8
  414.7 3.0 add.211
  419.3 6.1 collective-permute-start.7
  429.6 2.9 add.224
  437.4 2.9 add.213
  440.3 4.3 convolution_convert_fusion.3
  460.1 6.8 convolution_convert_fusion
  468.1 6.6 convolution_convert_fusion.17
  481.1 11.4 %collective-permute-start.6 = (bf16[256,2048]{1,0:T(8,128)(2,1)S(1)}, bf16[256,2048]{1,0:T(8,128)(2,1)S(1)}, u32[]{:S(2)}, u32[]{:S(2)}) collective-permute-start(bf16[256,2048]{1,0:T(8,128)(2,1)S(1)} %copy-done.22), channel_id=1, source_target_pairs={{0,1},{3,2},{4,5},{7,6},{8,9},{11,10},{12,13},{15,14},{16,17},{19,... | collective-permute-start | bytes 3145736 | tf_op jit(solution)/shard_map/ppermute | solution.py:188
  493.8 5.0 convolution_convert_fusion.6
  498.8 3.8 collective-permute-start.10
  507.4 8.6 %collective-permute-done.6 = bf16[256,2048]{1,0:T(8,128)(2,1)S(1)} collective-permute-done((bf16[256,2048]{1,0:T(8,128)(2,1)S(1)}, bf16[256,2048]{1,0:T(8,128)(2,1)S(1)}, u32[]{:S(2)}, u32[]{:S(2)}) %collective-permute-start.6) | collective-permute-done | bytes 1048608 | tf_op jit(solution)/shard_map/ppermute | solution.py:188
  519.4 19.1 %collective-permute-done.5 = bf16[256,2048]{1,0:T(8,128)(2,1)S(1)} collective-permute-done((bf16[256,2048]{1,0:T(8,128)(2,1)S(1)}, bf16[256,2048]{1,0:T(8,128)(2,1)S(1)}, u32[]{:S(2)}, u32[]{:S(2)}) %collective-permute-start.5) | collective-permute-done | bytes 1048608 | tf_op jit(solution)/shard_map/ppermute | solution.py:188
  540.9 18.1 %collective-permute-done.10 = bf16[256,2048]{1,0:T(8,128)(2,1)S(1)} collective-permute-done((bf16[256,2048]{1,0:T(8,128)(2,1)S(1)}, bf16[256,2048]{1,0:T(8,128)(2,1)S(1)}, u32[]{:S(2)}, u32[]{:S(2)}) %collective-permute-start.10) | collective-permute-done | bytes 1048608 | tf_op jit(solution)/shard_map/ppermute | solution.py:188
  561.0 8.7 %collective-permute-done.37 = bf16[256,2048]{1,0:T(8,128)(2,1)S(1)} collective-permute-done((bf16[256,2048]{1,0:T(8,128)(2,1)S(1)}, bf16[256,2048]{1,0:T(8,128)(2,1)S(1)}, u32[]{:S(2)}, u32[]{:S(2)}) %collective-permute-start.37) | collective-permute-done | bytes 1048608 | tf_op jit(solution)/shard_map/ppermute | solution.py:188
  571.2 19.0 %collective-permute-done.36 = bf16[256,2048]{1,0:T(8,128)(2,1)S(1)} collective-permute-done((bf16[256,2048]{1,0:T(8,128)(2,1)S(1)}, bf16[256,2048]{1,0:T(8,128)(2,1)S(1)}, u32[]{:S(2)}, u32[]{:S(2)}) %collective-permute-start.36) | collective-permute-done | bytes 1048608 | tf_op jit(solution)/shard_map/ppermute | solution.py:188
  600.2 14.9 %collective-permute-done.8 = bf16[256,2048]{1,0:T(8,128)(2,1)S(1)} collective-permute-done((bf16[256,2048]{1,0:T(8,128)(2,1)S(1)}, bf16[256,2048]{1,0:T(8,128)(2,1)S(1)}, u32[]{:S(2)}, u32[]{:S(2)}) %collective-permute-start.8) | collective-permute-done | bytes 1048608 | tf_op jit(solution)/shard_map/ppermute | solution.py:188
  616.3 18.6 %collective-permute-done.13 = bf16[256,2048]{1,0:T(8,128)(2,1)S(1)} collective-permute-done((bf16[256,2048]{1,0:T(8,128)(2,1)S(1)}, bf16[256,2048]{1,0:T(8,128)(2,1)S(1)}, u32[]{:S(2)}, u32[]{:S(2)}) %collective-permute-start.13) | collective-permute-done | bytes 1048608 | tf_op jit(solution)/shard_map/ppermute | solution.py:188
  636.1 4.6 maximum_convert_fusion
  642.9 6.4 convolution_convert_fusion.4
  649.3 9.9 %collective-permute-start.11 = (bf16[2048,384]{1,0:T(8,128)(2,1)}, bf16[2048,384]{1,0:T(8,128)(2,1)}, u32[]{:S(2)}, u32[]{:S(2)}) collective-permute-start(bf16[2048,384]{1,0:T(8,128)(2,1)} %convolution_convert_fusion.4), channel_id=1, source_target_pairs={{0,1},{3,2},{4,5},{7,6},{8,9},{11,10},{12,13},{15,14},{16,17},{19,... | collective-permute-start | bytes 4718600 | tf_op jit(solution)/shard_map/ppermute | solution.py:188
  670.1 19.9 %collective-permute-start.12 = (bf16[128,2048]{1,0:T(8,128)(2,1)}, bf16[128,2048]{1,0:T(8,128)(2,1)S(1)}, u32[]{:S(2)}, u32[]{:S(2)}) collective-permute-start(bf16[128,2048]{1,0:T(8,128)(2,1)} %reduce-scatter.11.cloned.1.call-done), channel_id=1, source_target_pairs={{0,1},{3,2},{4,5},{7,6},{8,9},{11,10},{12,13},{15,14},{16,17},{19,... | collective-permute-start | bytes 1572872 | tf_op jit(solution)/shard_map/ppermute | solution.py:188
  690.0 2.6 constant_dynamic-update-slice_fusion.8
  692.7 7.6 collective-permute-done.12
  704.5 2.6 constant_dynamic-update-slice_fusion.7
  707.2 5.6 collective-permute-done.31
  712.8 2.6 constant_dynamic-update-slice_fusion.6
  715.4 15.5 %collective-permute-done.30 = bf16[256,2048]{1,0:T(8,128)(2,1)} collective-permute-done((bf16[256,2048]{1,0:T(8,128)(2,1)}, bf16[256,2048]{1,0:T(8,128)(2,1)}, u32[]{:S(2)}, u32[]{:S(2)}) %collective-permute-start.30) | collective-permute-done | bytes 1048608 | tf_op jit(solution)/shard_map/ppermute | solution.py:188
  731.6 2.6 constant_dynamic-update-slice_fusion.5
  738.5 11.8 %fusion.109 = (f32[2048,1024]{1,0:T(8,128)}, f32[2048,1024]{1,0:T(8,128)}) fusion(bf16[2048,2048]{1,0:T(8,128)(2,1)} %constant_dynamic-update-slice_fusion.5), kind=kLoop, calls=%fused_computation.215 | loop fusion | bytes 33554432 | tf_op jit(solution)/shard_map/slice | solution.py:330
  751.0 16.7 %collective-permute-done.29 = bf16[128,2048]{1,0:T(8,128)(2,1)S(1)} collective-permute-done((bf16[128,2048]{1,0:T(8,128)(2,1)S(1)}, bf16[128,2048]{1,0:T(8,128)(2,1)S(1)}, u32[]{:S(2)}, u32[]{:S(2)}) %collective-permute-start.29) | collective-permute-done | bytes 524320 | tf_op jit(solution)/shard_map/ppermute | solution.py:188
  768.8 29.0 %collective-permute-done.28 = bf16[2048,384]{1,0:T(8,128)(2,1)} collective-permute-done((bf16[2048,384]{1,0:T(8,128)(2,1)}, bf16[2048,384]{1,0:T(8,128)(2,1)}, u32[]{:S(2)}, u32[]{:S(2)}) %collective-permute-start.28) | collective-permute-done | bytes 1572896 | tf_op jit(solution)/shard_map/ppermute | solution.py:188
  803.1 38.3 %psum.7 = f32[4104]{0:T(1024)S(1)} all-reduce(f32[4104]{0:T(1024)S(1)} %pad_maximum_fusion.6), channel_id=1, replica_groups=mesh['heads'=8,'batch'=4] {'heads','batch'}, use_global_device_ids=true, to_apply=%region_23.24 | all-reduce | flops 4104 | bytes 32832 | tf_op jit(solution)/shard_map/psum | solution.py:316
  842.5 3.3 fusion.11
  (344 shorter events, 134.3 us)
Async XLA Ops:
  7.2 59.8 %all-gather.5.cloned.1.call-start = ((), (), s32[]{:S(2)}) async-start(), calls=%async_computation.5 | async-start | bytes 9437184 | tf_op jit(solution)/shard_map/all_gather | solution.py:246
  7.9 97.7 %all-gather.9.cloned.1.call-start = ((), (), s32[]{:S(2)}) async-start(), calls=%async_computation.7 | async-start | bytes 4718592 | tf_op jit(solution)/shard_map/all_gather | solution.py:246
  8.7 136.9 %all-gather.7.cloned.1.call-start = ((), (), s32[]{:S(2)}) async-start(), calls=%async_computation.6 | async-start | bytes 4718592 | tf_op jit(solution)/shard_map/all_gather | solution.py:271
  10.8 71.9 %copy-start.56 = (s32[2,512]{1,0:T(2,128)}, s32[2,512]{1,0:T(2,128)S(1)}, u32[]{:S(2)}) copy-start(s32[2,512]{1,0:T(2,128)S(1)} %get-tuple-element.266) | copy-start | bytes 12292
  10.8 74.2 %copy-start.54 = (s32[2,512]{1,0:T(2,128)}, s32[2,512]{1,0:T(2,128)S(1)}, u32[]{:S(2)}) copy-start(s32[2,512]{1,0:T(2,128)S(1)} %get-tuple-element.265) | copy-start | bytes 12292
  13.5 69.2 %copy-start.58 = (pred[2,512]{1,0:T(4,128)(4,1)}, pred[2,512]{1,0:T(4,128)(4,1)S(1)}, u32[]{:S(2)}) copy-start(pred[2,512]{1,0:T(4,128)(4,1)S(1)} %get-tuple-element.268) | copy-start | bytes 3076
  14.7 57.6 %copy-start.37 = (bf16[2048,384]{1,0:T(8,128)(2,1)}, bf16[2048,384]{1,0:T(8,128)(2,1)S(1)}, u32[]{:S(2)}) copy-start(bf16[2048,384]{1,0:T(8,128)(2,1)S(1)} %constant_dynamic-update-slice_fusion) | copy-start | bytes 4718596
  16.1 56.1 %copy-start.41 = (f32[2048]{0:T(1024)S(1)}, f32[2048]{0:T(1024)}, u32[]{:S(2)}) copy-start(f32[2048]{0:T(1024)} %param.25) | copy-start | bytes 24580
  92.6 109.2 %all-gather.11.cloned.1.call-start = ((), (), s32[]{:S(2)}) async-start(), calls=%async_computation.9 | async-start | bytes 9437184 | tf_op jit(solution)/shard_map/all_gather | solution.py:246
  93.2 243.6 %reduce-scatter.7.cloned.1.call-start = ((), (), s32[]{:S(2)}) async-start(), calls=%async_computation.10 | async-start | bytes 9437184 | tf_op jit(solution)/shard_map/reduce_scatter | solution.py:249
  100.5 64.4 %copy-start.39 = (f32[2048]{0:T(1024)S(1)}, f32[2048]{0:T(1024)}, u32[]{:S(2)}) copy-start(f32[2048]{0:T(1024)} %param.26) | copy-start | bytes 24580
  249.5 147.0 %reduce-scatter.5.cloned.1.call-start = ((), (), s32[]{:S(2)}) async-start(), calls=%async_computation.8 | async-start | bytes 9437184 | tf_op jit(solution)/shard_map/reduce_scatter | solution.py:249
  266.3 19.2 %slice-start.2 = ((s8[8388608]{0:T(1024)(128)(4,1)}), s8[4194304]{0:T(1024)(128)(4,1)S(1)}, s32[]{:S(2)}) async-start(s8[8388608]{0:T(1024)(128)(4,1)} %bitcast.109), calls=%async_computation.15 | async-start | bytes 8388608
  272.5 13.0 %slice-start.3 = ((s8[8388608]{0:T(1024)(128)(4,1)}), s8[4194304]{0:T(1024)(128)(4,1)S(1)}, s32[]{:S(2)}) async-start(s8[8388608]{0:T(1024)(128)(4,1)} %bitcast.109), calls=%async_computation.16 | async-start | bytes 8388608
  272.6 53.3 %collective-permute-start.1 = (bf16[256,2048]{1,0:T(8,128)(2,1)S(1)}, bf16[256,2048]{1,0:T(8,128)(2,1)S(1)}, u32[]{:S(2)}, u32[]{:S(2)}) collective-permute-start(bf16[256,2048]{1,0:T(8,128)(2,1)S(1)} %convolution_convert_fusion.13), channel_id=1, source_target_pairs={{0,1},{3,2},{4,5},{7,6},{8,9},{11,10},{12,13},{15,14},{16,17},{19,... | collective-permute-start | bytes 3145736 | tf_op jit(solution)/shard_map/ppermute | solution.py:188
  282.9 45.1 %collective-permute-start = (bf16[256,2048]{1,0:T(8,128)(2,1)S(1)}, bf16[256,2048]{1,0:T(8,128)(2,1)S(1)}, u32[]{:S(2)}, u32[]{:S(2)}) collective-permute-start(bf16[256,2048]{1,0:T(8,128)(2,1)S(1)} %convolution_convert_fusion.14), channel_id=1, source_target_pairs={{0,1},{3,2},{4,5},{7,6},{8,9},{11,10},{12,13},{15,14},{16,17},{19,... | collective-permute-start | bytes 3145736 | tf_op jit(solution)/shard_map/ppermute | solution.py:188
  317.2 97.5 %collective-permute-start.4 = (bf16[256,2048]{1,0:T(8,128)(2,1)}, bf16[256,2048]{1,0:T(8,128)(2,1)}, u32[]{:S(2)}, u32[]{:S(2)}) collective-permute-start(bf16[256,2048]{1,0:T(8,128)(2,1)} %convolution_convert_fusion.11), channel_id=1, source_target_pairs={{0,1},{3,2},{4,5},{7,6},{8,9},{11,10},{12,13},{15,14},{16,17},{19,... | collective-permute-start | bytes 3145736 | tf_op jit(solution)/shard_map/ppermute | solution.py:188
  326.4 93.0 %collective-permute-start.27 = (bf16[256,2048]{1,0:T(8,128)(2,1)S(1)}, bf16[256,2048]{1,0:T(8,128)(2,1)}, u32[]{:S(2)}, u32[]{:S(2)}) collective-permute-start(bf16[256,2048]{1,0:T(8,128)(2,1)S(1)} %add.209), channel_id=1, source_target_pairs={{1,2},{2,1},{5,6},{6,5},{9,10},{10,9},{13,14},{14,13},{17,18},{18,... | collective-permute-start | bytes 3145736 | tf_op jit(solution)/shard_map/ppermute | solution.py:188
  329.4 98.7 %collective-permute-start.26 = (bf16[256,2048]{1,0:T(8,128)(2,1)}, bf16[256,2048]{1,0:T(8,128)(2,1)}, u32[]{:S(2)}, u32[]{:S(2)}) collective-permute-start(bf16[256,2048]{1,0:T(8,128)(2,1)} %add.210), channel_id=1, source_target_pairs={{1,2},{2,1},{5,6},{6,5},{9,10},{10,9},{13,14},{14,13},{17,18},{18,... | collective-permute-start | bytes 3145736 | tf_op jit(solution)/shard_map/ppermute | solution.py:188
  331.0 101.5 %collective-permute-start.3 = (bf16[256,2048]{1,0:T(8,128)(2,1)}, bf16[256,2048]{1,0:T(8,128)(2,1)}, u32[]{:S(2)}, u32[]{:S(2)}) collective-permute-start(bf16[256,2048]{1,0:T(8,128)(2,1)} %convolution_convert_fusion.12), channel_id=1, source_target_pairs={{0,1},{3,2},{4,5},{7,6},{8,9},{11,10},{12,13},{15,14},{16,17},{19,... | collective-permute-start | bytes 3145736 | tf_op jit(solution)/shard_map/ppermute | solution.py:188
  334.4 101.3 %collective-permute-start.2 = (bf16[256,2048]{1,0:T(8,128)(2,1)}, bf16[256,2048]{1,0:T(8,128)(2,1)}, u32[]{:S(2)}, u32[]{:S(2)}) collective-permute-start(bf16[256,2048]{1,0:T(8,128)(2,1)} %convolution_convert_fusion.15), channel_id=1, source_target_pairs={{0,1},{3,2},{4,5},{7,6},{8,9},{11,10},{12,13},{15,14},{16,17},{19,... | collective-permute-start | bytes 3145736 | tf_op jit(solution)/shard_map/ppermute | solution.py:188
  403.4 41.4 %all-to-all-start = ((bf16[256,8,128]{2,0,1:T(8,128)(2,1)}), bf16[256,8,128]{2,0,1:T(8,128)(2,1)}, u32[]{:S(2)}, u32[]{:S(2)}) async-start(bf16[256,8,128]{2,0,1:T(8,128)(2,1)} %bitcast.119), calls=%async_computation.2 | async-start | bytes 1048576 | tf_op jit(solution)/shard_map/all_to_all | solution.py:304
  407.5 262.6 %reduce-scatter.11.cloned.1.call-start = ((), (), s32[]{:S(2)}) async-start(), calls=%async_computation.12 | async-start | bytes 4718592 | tf_op jit(solution)/shard_map/reduce_scatter | solution.py:249
  417.7 49.3 %collective-permute-start.25 = (bf16[256,2048]{1,0:T(8,128)(2,1)}, bf16[256,2048]{1,0:T(8,128)(2,1)}, u32[]{:S(2)}, u32[]{:S(2)}) collective-permute-start(bf16[256,2048]{1,0:T(8,128)(2,1)} %add.211), channel_id=1, source_target_pairs={{1,2},{2,1},{5,6},{6,5},{9,10},{10,9},{13,14},{14,13},{17,18},{18,... | collective-permute-start | bytes 3145736 | tf_op jit(solution)/shard_map/ppermute | solution.py:188
  419.3 57.5 %collective-permute-start.7 = (bf16[256,2048]{1,0:T(8,128)(2,1)}, bf16[256,2048]{1,0:T(8,128)(2,1)}, u32[]{:S(2)}, u32[]{:S(2)}) collective-permute-start(bf16[256,2048]{1,0:T(8,128)(2,1)} %convolution_convert_fusion.9), channel_id=1, source_target_pairs={{0,1},{3,2},{4,5},{7,6},{8,9},{11,10},{12,13},{15,14},{16,17},{19,... | collective-permute-start | bytes 3145736 | tf_op jit(solution)/shard_map/ppermute | solution.py:188
  428.1 52.1 %collective-permute-start.41 = (bf16[256,2048]{1,0:T(8,128)(2,1)}, bf16[256,2048]{1,0:T(8,128)(2,1)}, u32[]{:S(2)}, u32[]{:S(2)}) collective-permute-start(bf16[256,2048]{1,0:T(8,128)(2,1)} %add.223), channel_id=1, source_target_pairs={{1,0},{2,3},{5,4},{6,7},{9,8},{10,11},{13,12},{14,15},{17,16},{18,... | collective-permute-start | bytes 3145736 | tf_op jit(solution)/shard_map/ppermute | solution.py:188
  432.5 48.6 %collective-permute-start.40 = (bf16[256,2048]{1,0:T(8,128)(2,1)}, bf16[256,2048]{1,0:T(8,128)(2,1)}, u32[]{:S(2)}, u32[]{:S(2)}) collective-permute-start(bf16[256,2048]{1,0:T(8,128)(2,1)} %add.224), channel_id=1, source_target_pairs={{1,0},{2,3},{5,4},{6,7},{9,8},{10,11},{13,12},{14,15},{17,16},{18,... | collective-permute-start | bytes 3145736 | tf_op jit(solution)/shard_map/ppermute | solution.py:188
  435.7 56.8 %collective-permute-start.24 = (bf16[256,2048]{1,0:T(8,128)(2,1)S(1)}, bf16[256,2048]{1,0:T(8,128)(2,1)}, u32[]{:S(2)}, u32[]{:S(2)}) collective-permute-start(bf16[256,2048]{1,0:T(8,128)(2,1)S(1)} %add.212), channel_id=1, source_target_pairs={{1,2},{2,1},{5,6},{6,5},{9,10},{10,9},{13,14},{14,13},{17,18},{18,... | collective-permute-start | bytes 3145736 | tf_op jit(solution)/shard_map/ppermute | solution.py:188
  444.7 356.5 %reduce-scatter.9.cloned.1.call-start = ((), (), s32[]{:S(2)}) async-start(), calls=%async_computation.11 | async-start | bytes 9437184 | tf_op jit(solution)/shard_map/reduce_scatter | solution.py:249
  467.0 31.9 %collective-permute-start.23 = (bf16[256,2048]{1,0:T(8,128)(2,1)}, bf16[256,2048]{1,0:T(8,128)(2,1)S(1)}, u32[]{:S(2)}, u32[]{:S(2)}) collective-permute-start(bf16[256,2048]{1,0:T(8,128)(2,1)} %add.213), channel_id=1, source_target_pairs={{1,2},{2,1},{5,6},{6,5},{9,10},{10,9},{13,14},{14,13},{17,18},{18,... | collective-permute-start | bytes 3145736 | tf_op jit(solution)/shard_map/ppermute | solution.py:188
  474.7 17.8 %copy-start.21 = (bf16[256,2048]{1,0:T(8,128)(2,1)S(1)}, bf16[256,2048]{1,0:T(8,128)(2,1)}, u32[]{:S(2)}) copy-start(bf16[256,2048]{1,0:T(8,128)(2,1)} %convolution_convert_fusion.16) | copy-start | bytes 3145732
  474.7 19.1 %copy-start.65 = (bf16[2048,1024]{0,1:T(8,128)(2,1)S(1)}, bf16[2048,1024]{0,1:T(8,128)(2,1)}, u32[]{:S(2)}) copy-start(bf16[2048,1024]{0,1:T(8,128)(2,1)} %copy-done.63) | copy-start | bytes 12582916
  476.8 41.3 %collective-permute-start.39 = (bf16[256,2048]{1,0:T(8,128)(2,1)S(1)}, bf16[256,2048]{1,0:T(8,128)(2,1)S(1)}, u32[]{:S(2)}, u32[]{:S(2)}) collective-permute-start(bf16[256,2048]{1,0:T(8,128)(2,1)S(1)} %add.225), channel_id=1, source_target_pairs={{1,0},{2,3},{5,4},{6,7},{9,8},{10,11},{13,12},{14,15},{17,16},{18,... | collective-permute-start | bytes 3145736 | tf_op jit(solution)/shard_map/ppermute | solution.py:188
  480.2 18.7 %copy-start.19 = (bf16[256,2048]{1,0:T(8,128)(2,1)S(1)}, bf16[256,2048]{1,0:T(8,128)(2,1)}, u32[]{:S(2)}) copy-start(bf16[256,2048]{1,0:T(8,128)(2,1)} %convolution_convert_fusion.7) | copy-start | bytes 3145732
  480.2 25.9 %collective-permute-start.22 = (bf16[256,2048]{1,0:T(8,128)(2,1)S(1)}, bf16[256,2048]{1,0:T(8,128)(2,1)S(1)}, u32[]{:S(2)}, u32[]{:S(2)}) collective-permute-start(bf16[256,2048]{1,0:T(8,128)(2,1)S(1)} %add.214), channel_id=1, source_target_pairs={{1,2},{2,1},{5,6},{6,5},{9,10},{10,9},{13,14},{14,13},{17,18},{18,... | collective-permute-start | bytes 3145736 | tf_op jit(solution)/shard_map/ppermute | solution.py:188
  481.1 34.9 %collective-permute-start.6 = (bf16[256,2048]{1,0:T(8,128)(2,1)S(1)}, bf16[256,2048]{1,0:T(8,128)(2,1)S(1)}, u32[]{:S(2)}, u32[]{:S(2)}) collective-permute-start(bf16[256,2048]{1,0:T(8,128)(2,1)S(1)} %copy-done.22), channel_id=1, source_target_pairs={{0,1},{3,2},{4,5},{7,6},{8,9},{11,10},{12,13},{15,14},{16,17},{19,... | collective-permute-start | bytes 3145736 | tf_op jit(solution)/shard_map/ppermute | solution.py:188
  492.5 46.0 %collective-permute-start.5 = (bf16[256,2048]{1,0:T(8,128)(2,1)S(1)}, bf16[256,2048]{1,0:T(8,128)(2,1)S(1)}, u32[]{:S(2)}, u32[]{:S(2)}) collective-permute-start(bf16[256,2048]{1,0:T(8,128)(2,1)S(1)} %copy-done.21), channel_id=1, source_target_pairs={{0,1},{3,2},{4,5},{7,6},{8,9},{11,10},{12,13},{15,14},{16,17},{19,... | collective-permute-start | bytes 3145736 | tf_op jit(solution)/shard_map/ppermute | solution.py:188
  498.8 60.2 %collective-permute-start.10 = (bf16[256,2048]{1,0:T(8,128)(2,1)S(1)}, bf16[256,2048]{1,0:T(8,128)(2,1)S(1)}, u32[]{:S(2)}, u32[]{:S(2)}) collective-permute-start(bf16[256,2048]{1,0:T(8,128)(2,1)S(1)} %copy-done.19), channel_id=1, source_target_pairs={{0,1},{3,2},{4,5},{7,6},{8,9},{11,10},{12,13},{15,14},{16,17},{19,... | collective-permute-start | bytes 3145736 | tf_op jit(solution)/shard_map/ppermute | solution.py:188
  506.1 54.2 %collective-permute-start.38 = (bf16[256,2048]{1,0:T(8,128)(2,1)S(1)}, bf16[256,2048]{1,0:T(8,128)(2,1)S(1)}, u32[]{:S(2)}, u32[]{:S(2)}) collective-permute-start(bf16[256,2048]{1,0:T(8,128)(2,1)S(1)} %add.226), channel_id=1, source_target_pairs={{1,0},{2,3},{5,4},{6,7},{9,8},{10,11},{13,12},{14,15},{17,16},{18,... | collective-permute-start | bytes 3145736 | tf_op jit(solution)/shard_map/ppermute | solution.py:188
  516.0 53.7 %collective-permute-start.37 = (bf16[256,2048]{1,0:T(8,128)(2,1)S(1)}, bf16[256,2048]{1,0:T(8,128)(2,1)S(1)}, u32[]{:S(2)}, u32[]{:S(2)}) collective-permute-start(bf16[256,2048]{1,0:T(8,128)(2,1)S(1)} %add.227), channel_id=1, source_target_pairs={{1,0},{2,3},{5,4},{6,7},{9,8},{10,11},{13,12},{14,15},{17,16},{18,... | collective-permute-start | bytes 3145736 | tf_op jit(solution)/shard_map/ppermute | solution.py:188
  518.1 72.0 %collective-permute-start.36 = (bf16[256,2048]{1,0:T(8,128)(2,1)S(1)}, bf16[256,2048]{1,0:T(8,128)(2,1)S(1)}, u32[]{:S(2)}, u32[]{:S(2)}) collective-permute-start(bf16[256,2048]{1,0:T(8,128)(2,1)S(1)} %add.228), channel_id=1, source_target_pairs={{1,0},{2,3},{5,4},{6,7},{9,8},{10,11},{13,12},{14,15},{17,16},{18,... | collective-permute-start | bytes 3145736 | tf_op jit(solution)/shard_map/ppermute | solution.py:188
  538.5 53.2 %collective-permute-start.21 = (bf16[256,2048]{1,0:T(8,128)(2,1)S(1)}, bf16[256,2048]{1,0:T(8,128)(2,1)S(1)}, u32[]{:S(2)}, u32[]{:S(2)}) collective-permute-start(bf16[256,2048]{1,0:T(8,128)(2,1)S(1)} %add.215), channel_id=1, source_target_pairs={{1,2},{2,1},{5,6},{6,5},{9,10},{10,9},{13,14},{14,13},{17,18},{18,... | collective-permute-start | bytes 3145736 | tf_op jit(solution)/shard_map/ppermute | solution.py:188
  540.5 29.1 %copy-start.20 = (bf16[256,2048]{1,0:T(8,128)(2,1)S(1)}, bf16[256,2048]{1,0:T(8,128)(2,1)}, u32[]{:S(2)}) copy-start(bf16[256,2048]{1,0:T(8,128)(2,1)} %convolution_convert_fusion.8) | copy-start | bytes 3145732
  559.0 34.5 %collective-permute-start.20 = (bf16[256,2048]{1,0:T(8,128)(2,1)S(1)}, bf16[256,2048]{1,0:T(8,128)(2,1)S(1)}, u32[]{:S(2)}, u32[]{:S(2)}) collective-permute-start(bf16[256,2048]{1,0:T(8,128)(2,1)S(1)} %add.216), channel_id=1, source_target_pairs={{1,2},{2,1},{5,6},{6,5},{9,10},{10,9},{13,14},{14,13},{17,18},{18,... | collective-permute-start | bytes 3145736 | tf_op jit(solution)/shard_map/ppermute | solution.py:188
  560.3 36.5 %collective-permute-start.19 = (bf16[256,2048]{1,0:T(8,128)(2,1)S(1)}, bf16[256,2048]{1,0:T(8,128)(2,1)S(1)}, u32[]{:S(2)}, u32[]{:S(2)}) collective-permute-start(bf16[256,2048]{1,0:T(8,128)(2,1)S(1)} %add.217), channel_id=1, source_target_pairs={{1,2},{2,1},{5,6},{6,5},{9,10},{10,9},{13,14},{14,13},{17,18},{18,... | collective-permute-start | bytes 3145736 | tf_op jit(solution)/shard_map/ppermute | solution.py:188
  569.7 28.9 %collective-permute-start.9 = (bf16[256,2048]{1,0:T(8,128)(2,1)S(1)}, bf16[256,2048]{1,0:T(8,128)(2,1)S(1)}, u32[]{:S(2)}, u32[]{:S(2)}) collective-permute-start(bf16[256,2048]{1,0:T(8,128)(2,1)S(1)} %copy-done.20), channel_id=1, source_target_pairs={{0,1},{3,2},{4,5},{7,6},{8,9},{11,10},{12,13},{15,14},{16,17},{19,... | collective-permute-start | bytes 3145736 | tf_op jit(solution)/shard_map/ppermute | solution.py:188
  590.1 25.0 %collective-permute-start.8 = (bf16[256,2048]{1,0:T(8,128)(2,1)S(1)}, bf16[256,2048]{1,0:T(8,128)(2,1)S(1)}, u32[]{:S(2)}, u32[]{:S(2)}) collective-permute-start(bf16[256,2048]{1,0:T(8,128)(2,1)S(1)} %convolution_convert_fusion.17), channel_id=1, source_target_pairs={{0,1},{3,2},{4,5},{7,6},{8,9},{11,10},{12,13},{15,14},{16,17},{19,... | collective-permute-start | bytes 3145736 | tf_op jit(solution)/shard_map/ppermute | solution.py:188
  591.6 43.3 %collective-permute-start.13 = (bf16[256,2048]{1,0:T(8,128)(2,1)S(1)}, bf16[256,2048]{1,0:T(8,128)(2,1)S(1)}, u32[]{:S(2)}, u32[]{:S(2)}) collective-permute-start(bf16[256,2048]{1,0:T(8,128)(2,1)S(1)} %convolution_convert_fusion.6), channel_id=1, source_target_pairs={{0,1},{3,2},{4,5},{7,6},{8,9},{11,10},{12,13},{15,14},{16,17},{19,... | collective-permute-start | bytes 3145736 | tf_op jit(solution)/shard_map/ppermute | solution.py:188
  593.6 48.6 %collective-permute-start.35 = (bf16[256,2048]{1,0:T(8,128)(2,1)S(1)}, bf16[256,2048]{1,0:T(8,128)(2,1)S(1)}, u32[]{:S(2)}, u32[]{:S(2)}) collective-permute-start(bf16[256,2048]{1,0:T(8,128)(2,1)S(1)} %add.229), channel_id=1, source_target_pairs={{1,0},{2,3},{5,4},{6,7},{9,8},{10,11},{13,12},{14,15},{17,16},{18,... | collective-permute-start | bytes 3145736 | tf_op jit(solution)/shard_map/ppermute | solution.py:188
  596.8 52.5 %collective-permute-start.34 = (bf16[256,2048]{1,0:T(8,128)(2,1)S(1)}, bf16[256,2048]{1,0:T(8,128)(2,1)S(1)}, u32[]{:S(2)}, u32[]{:S(2)}) collective-permute-start(bf16[256,2048]{1,0:T(8,128)(2,1)S(1)} %add.230), channel_id=1, source_target_pairs={{1,0},{2,3},{5,4},{6,7},{9,8},{10,11},{13,12},{14,15},{17,16},{18,... | collective-permute-start | bytes 3145736 | tf_op jit(solution)/shard_map/ppermute | solution.py:188
  598.5 66.2 %collective-permute-start.33 = (bf16[256,2048]{1,0:T(8,128)(2,1)S(1)}, bf16[256,2048]{1,0:T(8,128)(2,1)S(1)}, u32[]{:S(2)}, u32[]{:S(2)}) collective-permute-start(bf16[256,2048]{1,0:T(8,128)(2,1)S(1)} %add.231), channel_id=1, source_target_pairs={{1,0},{2,3},{5,4},{6,7},{9,8},{10,11},{13,12},{14,15},{17,16},{18,... | collective-permute-start | bytes 3145736 | tf_op jit(solution)/shard_map/ppermute | solution.py:188
  615.2 45.5 %collective-permute-start.18 = (bf16[256,2048]{1,0:T(8,128)(2,1)S(1)}, bf16[256,2048]{1,0:T(8,128)(2,1)S(1)}, u32[]{:S(2)}, u32[]{:S(2)}) collective-permute-start(bf16[256,2048]{1,0:T(8,128)(2,1)S(1)} %add.218), channel_id=1, source_target_pairs={{1,2},{2,1},{5,6},{6,5},{9,10},{10,9},{13,14},{14,13},{17,18},{18,... | collective-permute-start | bytes 3145736 | tf_op jit(solution)/shard_map/ppermute | solution.py:188
  615.9 27.0 %slice-start = ((s8[8388608]{0:T(1024)(128)(4,1)}), s8[4194304]{0:T(1024)(128)(4,1)S(1)}, s32[]{:S(2)}) async-start(s8[8388608]{0:T(1024)(128)(4,1)} %bitcast.107), calls=%async_computation.13 | async-start | bytes 8388608
  634.9 29.8 %collective-permute-start.17 = (bf16[256,2048]{1,0:T(8,128)(2,1)S(1)}, bf16[256,2048]{1,0:T(8,128)(2,1)S(1)}, u32[]{:S(2)}, u32[]{:S(2)}) collective-permute-start(bf16[256,2048]{1,0:T(8,128)(2,1)S(1)} %add.219), channel_id=1, source_target_pairs={{1,2},{2,1},{5,6},{6,5},{9,10},{10,9},{13,14},{14,13},{17,18},{18,... | collective-permute-start | bytes 3145736 | tf_op jit(solution)/shard_map/ppermute | solution.py:188
  642.1 25.3 %collective-permute-start.16 = (bf16[256,2048]{1,0:T(8,128)(2,1)S(1)}, bf16[256,2048]{1,0:T(8,128)(2,1)S(1)}, u32[]{:S(2)}, u32[]{:S(2)}) collective-permute-start(bf16[256,2048]{1,0:T(8,128)(2,1)S(1)} %add.220), channel_id=1, source_target_pairs={{1,2},{2,1},{5,6},{6,5},{9,10},{10,9},{13,14},{14,13},{17,18},{18,... | collective-permute-start | bytes 3145736 | tf_op jit(solution)/shard_map/ppermute | solution.py:188
  649.3 52.1 %collective-permute-start.11 = (bf16[2048,384]{1,0:T(8,128)(2,1)}, bf16[2048,384]{1,0:T(8,128)(2,1)}, u32[]{:S(2)}, u32[]{:S(2)}) collective-permute-start(bf16[2048,384]{1,0:T(8,128)(2,1)} %convolution_convert_fusion.4), channel_id=1, source_target_pairs={{0,1},{3,2},{4,5},{7,6},{8,9},{11,10},{12,13},{15,14},{16,17},{19,... | collective-permute-start | bytes 4718600 | tf_op jit(solution)/shard_map/ppermute | solution.py:188
  662.0 30.6 %collective-permute-start.32 = (bf16[256,2048]{1,0:T(8,128)(2,1)}, bf16[256,2048]{1,0:T(8,128)(2,1)}, u32[]{:S(2)}, u32[]{:S(2)}) collective-permute-start(bf16[256,2048]{1,0:T(8,128)(2,1)} %add.232), channel_id=1, source_target_pairs={{1,0},{2,3},{5,4},{6,7},{9,8},{10,11},{13,12},{14,15},{17,16},{18,... | collective-permute-start | bytes 3145736 | tf_op jit(solution)/shard_map/ppermute | solution.py:188
  666.1 46.7 %collective-permute-start.31 = (bf16[256,2048]{1,0:T(8,128)(2,1)}, bf16[256,2048]{1,0:T(8,128)(2,1)}, u32[]{:S(2)}, u32[]{:S(2)}) collective-permute-start(bf16[256,2048]{1,0:T(8,128)(2,1)} %add.233), channel_id=1, source_target_pairs={{1,0},{2,3},{5,4},{6,7},{9,8},{10,11},{13,12},{14,15},{17,16},{18,... | collective-permute-start | bytes 3145736 | tf_op jit(solution)/shard_map/ppermute | solution.py:188
  668.8 62.1 %collective-permute-start.30 = (bf16[256,2048]{1,0:T(8,128)(2,1)}, bf16[256,2048]{1,0:T(8,128)(2,1)}, u32[]{:S(2)}, u32[]{:S(2)}) collective-permute-start(bf16[256,2048]{1,0:T(8,128)(2,1)} %add.234), channel_id=1, source_target_pairs={{1,0},{2,3},{5,4},{6,7},{9,8},{10,11},{13,12},{14,15},{17,16},{18,... | collective-permute-start | bytes 3145736 | tf_op jit(solution)/shard_map/ppermute | solution.py:188
  670.1 30.2 %collective-permute-start.12 = (bf16[128,2048]{1,0:T(8,128)(2,1)}, bf16[128,2048]{1,0:T(8,128)(2,1)S(1)}, u32[]{:S(2)}, u32[]{:S(2)}) collective-permute-start(bf16[128,2048]{1,0:T(8,128)(2,1)} %reduce-scatter.11.cloned.1.call-done), channel_id=1, source_target_pairs={{0,1},{3,2},{4,5},{7,6},{8,9},{11,10},{12,13},{15,14},{16,17},{19,... | collective-permute-start | bytes 1572872 | tf_op jit(solution)/shard_map/ppermute | solution.py:188
  703.8 31.9 %collective-permute-start.14 = (bf16[2048,384]{1,0:T(8,128)(2,1)S(1)}, bf16[2048,384]{1,0:T(8,128)(2,1)S(1)}, u32[]{:S(2)}, u32[]{:S(2)}) collective-permute-start(bf16[2048,384]{1,0:T(8,128)(2,1)S(1)} %add.222), channel_id=1, source_target_pairs={{1,2},{2,1},{5,6},{6,5},{9,10},{10,9},{13,14},{14,13},{17,18},{18,... | collective-permute-start | bytes 4718600 | tf_op jit(solution)/shard_map/ppermute | solution.py:188
  730.9 3.3 collective-permute-start.15
  734.4 33.4 %collective-permute-start.29 = (bf16[128,2048]{1,0:T(8,128)(2,1)S(1)}, bf16[128,2048]{1,0:T(8,128)(2,1)S(1)}, u32[]{:S(2)}, u32[]{:S(2)}) collective-permute-start(bf16[128,2048]{1,0:T(8,128)(2,1)S(1)} %add.235), channel_id=1, source_target_pairs={{1,0},{2,3},{5,4},{6,7},{9,8},{10,11},{13,12},{14,15},{17,16},{18,... | collective-permute-start | bytes 1572872 | tf_op jit(solution)/shard_map/ppermute | solution.py:188
  737.2 60.6 %collective-permute-start.28 = (bf16[2048,384]{1,0:T(8,128)(2,1)}, bf16[2048,384]{1,0:T(8,128)(2,1)}, u32[]{:S(2)}, u32[]{:S(2)}) collective-permute-start(bf16[2048,384]{1,0:T(8,128)(2,1)} %add.236), channel_id=1, source_target_pairs={{1,0},{2,3},{5,4},{6,7},{9,8},{10,11},{13,12},{14,15},{17,16},{18,... | collective-permute-start | bytes 4718600 | tf_op jit(solution)/shard_map/ppermute | solution.py:188
  (60 other events, 250.7 us)
Sparse Core Ops, SparseCore 0:
  9.9 57.0 all-gather.4
  68.9 36.7 all-gather.8
  108.1 37.4 all-gather.6
  147.3 54.3 all-gather.10
  249.7 71.2 reduce-scatter.6
  325.2 71.2 reduce-scatter.4
  444.8 55.6 reduce-scatter.10
  504.3 71.2 reduce-scatter.8
where the time goes:
time: 862 us; the launch traced here: 853 us
  waiting for transfers between devices  344 us (40%)
  matrix products  207 us (24%)
  starting transfers between devices  109 us (13%)
  other arithmetic  95.5 us (11%)
  local copies, waits for them, and re-layouts  41.4 us (5%)
  blocking collectives  38.3 us (4%)
  between operations  17.7 us (2%)
    ppermute x42, waiting for transfers between devices, add(): arrived = lax.ppermute(array, self.axis, pairs)  182 us
    ppermute x42, starting transfers between devices, add(): arrived = lax.ppermute(array, self.axis, pairs)  104 us
    dot_general x14, matrix products, dot_cols(): lax.dot_general(left_mat, right_mat, (((0,), (0,)), ((), ())), preferred_...  78.3 us
    all_gather x3, waiting for transfers between devices, gather(): return lax.all_gather(array, 'heads', axis=0, tiled=True)  64.1 us
    reduce_scatter x4, waiting for transfers between devices, scatter(): return lax.psum_scatter(array, 'heads', scatter_dimension=0, tiled=True)  56.7 us
    dot_general x4, matrix products, dot_rows(): lax.dot_general(left_mat, right_mat, (((1,), (1,)), ((), ())), preferred_...  53.9 us
    all_gather x1, waiting for transfers between devices, per_device(): mixed_all = lax.all_gather(mixed, 'heads', axis=1, tiled=True)  39.9 us
    psum x1, blocking collectives, per_device(): lax.psum(jnp.concatenate([gain_attn_part, gain_mlp_part, slots]), ('heads...  38.3 us
  transfers between devices with their start and end apart: 51, of which 17 were waited for; matrix products, arithmetic and copies ran while one was open for 33% of the time, Pallas kernels for 0%

commit v1 on v0

--- a/solution.py
+++ b/solution.py
@@ -313,7 +313,9 @@
     d_x, gain_attn_part = norm_back(x_own, norm_scale(x_own), norm_attn, d_h1)
     grad_tokens = (d_x + d_y1).reshape(tokens.shape)
     slots = jnp.where(jnp.arange(n_heads) == here, d_share, 0.0)
-    sums = lax.psum(jnp.concatenate([gain_attn_part, gain_mlp_part, slots]), ("heads", "batch"))
+    sums = lax.psum(
+        lax.psum(jnp.concatenate([gain_attn_part, gain_mlp_part, slots]), "batch"), "heads"
+    )
     grad_mix = lax.dynamic_slice_in_dim(sums, 2 * width + here, 1, 0)
     wide = jnp.float32
     grad_qkv = grad_qkv.astype(wide)

time: 862 us -> 864 us (level)
    psum x1 -> x2, blocking collectives: 38.3 us -> 40 us  [the longest x1 22.3 us: per_device(): lax.psum(lax.psum(jnp.concatenate([gain_attn_part, gain_mlp_part, slots])...]
where the time goes in v1:
time: 864 us; the launch traced here: 854 us
  waiting for transfers between devices  344 us (40%)
  matrix products  207 us (24%)
  starting transfers between devices  109 us (13%)
  other arithmetic  95.5 us (11%)
  local copies, waits for them, and re-layouts  41.4 us (5%)
  blocking collectives  40 us (5%)
  between operations  17.5 us (2%)
    ppermute x42, waiting for transfers between devices, add(): arrived = lax.ppermute(array, self.axis, pairs)  181 us
    ppermute x42, starting transfers between devices, add(): arrived = lax.ppermute(array, self.axis, pairs)  104 us
    dot_general x14, matrix products, dot_cols(): lax.dot_general(left_mat, right_mat, (((0,), (0,)), ((), ())), preferred_...  78.4 us
    all_gather x3, waiting for transfers between devices, gather(): return lax.all_gather(array, 'heads', axis=0, tiled=True)  64.1 us
    reduce_scatter x4, waiting for transfers between devices, scatter(): return lax.psum_scatter(array, 'heads', scatter_dimension=0, tiled=True)  56.7 us
    dot_general x4, matrix products, dot_rows(): lax.dot_general(left_mat, right_mat, (((1,), (1,)), ((), ())), preferred_...  53.8 us
    all_gather x1, waiting for transfers between devices, per_device(): mixed_all = lax.all_gather(mixed, 'heads', axis=1, tiled=True)  39.9 us
    add x28, other arithmetic, add(): array = array + arrived  34.3 us
  transfers between devices with their start and end apart: 51, of which 17 were waited for; matrix products, arithmetic and copies ran while one was open for 33% of the time, Pallas kernels for 0%

profile of v1, /device:TPU:0, one launch (start us, length us, event | category | flops | bytes accessed | tf_op | source)
XLA Modules:
  0.0 854.4 jit_solution(1524078281685677400)
XLA Ops:
  16.1 50.9 %all-gather.5.cloned.1.call-done = bf16[2048,2048]{1,0:T(8,128)(2,1)} async-done(((bf16[256,2048]{1,0:T(8,128)(2,1)}), bf16[2048,2048]{1,0:T(8,128)(2,1)}) %all-gather.5.cloned.1.call-update) | async-done | bytes 8388624 | tf_op jit(solution)/shard_map/all_gather | solution.py:246
  67.0 5.2 fusion.2
  72.8 4.8 convolution_convert_fusion.5
  87.3 2.9 fusion.56
  93.2 4.8 constant_dynamic-update-slice_fusion.4
  100.5 5.2 all-gather.9.cloned.1.call-done
  105.7 39.9 %all-gather.7.cloned.1.call-done = bf16[2048,1024]{1,0:T(8,128)(2,1)} async-done(((bf16[2048,128]{1,0:T(8,128)(2,1)}), bf16[2048,1024]{1,0:T(8,128)(2,1)}) %all-gather.7.cloned.1.call-update) | async-done | bytes 4194320 | tf_op jit(solution)/shard_map/all_gather | solution.py:271
  145.6 13.5 %multiply_reduce_fusion = (f32[2048]{0:T(1024)S(1)}, f32[2048,2048]{1,0:T(8,128)S(1)}) fusion(bf16[2048,1024]{1,0:T(8,128)(2,1)} %all-gather.7.cloned.1.call-done, bf16[1024,2048]{1,0:T(8,128)(2,1)} %all-gather.9.cloned.1.call-done, bf16[2048,2048]{1,0:T(8,128)(2,1)} %all-gather.5.cloned.1.call-done), kind=kOutput, calls=%fused_computation.9 | convolution fusion | flops 8606709760 | bytes 33562624 | tf_op jit(solution)/shard_map/dot_general | solution.py:273
  159.1 5.8 copy-done
  164.9 4.4 multiply_convert_fusion
  169.4 24.3 %fusion.125 = f32[2048,2048]{0,1:T(8,128)} fusion(bf16[2048,2048]{1,0:T(8,128)(2,1)} %multiply_convert_fusion, bf16[2048,2048]{1,0:T(8,128)(2,1)} %constant_dynamic-update-slice_fusion.3), kind=kOutput, calls=%fused_computation.223 | convolution fusion | flops 17179869184 | bytes 33554432 | tf_op jit(solution)/shard_map/dot_general | solution.py:277
  193.7 8.1 all-gather.11.cloned.1.call-done
  201.8 22.7 %multiply_convert_fusion.2 = (bf16[2048,1024]{0,1:T(8,128)(2,1)S(1)}, bf16[2048,1024]{0,1:T(8,128)(2,1)}, bf16[2048,1024]{0,1:T(8,128)(2,1)}) fusion(f32[2048,2048]{0,1:T(8,128)} %fusion.125, bf16[2048,2048]{1,0:T(8,128)(2,1)} %all-gather.11.cloned.1.call-done, bf16[1024,2048]{1,0:T(8,128)(2,1)} %param.24), kind=kOutput, calls=%fused_computation.12 | convolution fusion | flops 8623489024 | bytes 41943040 | tf_op jit(solution)/shard_map/dot_general | solution.py:16
  226.4 22.9 %convolution_convert_fusion.1 = bf16[2048,2048]{1,0:T(8,128)(2,1)} fusion(bf16[2048,2048]{1,0:T(8,128)(2,1)} %constant_dynamic-update-slice_fusion.3, bf16[2048,1024]{0,1:T(8,128)(2,1)} %get-tuple-element.249, bf16[2048,1024]{0,1:T(8,128)(2,1)S(1)} %get-tuple-element.248), kind=kOutput, calls=%fused_computation.16 | convolution fusion | flops 17200840704 | bytes 25165824 | tf_op jit(solution)/shard_map/dot_general | solution.py:16
  249.4 14.5 %convolution_convert_fusion.2 = bf16[2048,2048]{1,0:T(8,128)(2,1)} fusion(bf16[2048,1024]{0,1:T(8,128)(2,1)} %get-tuple-element.252, bf16[1024,2048]{1,0:T(8,128)(2,1)} %param.24), kind=kOutput, calls=%fused_computation.17 | convolution fusion | flops 8594128896 | bytes 16777216 | tf_op jit(solution)/shard_map/dot_general | solution.py:297
  266.2 6.2 convolution_convert_fusion.13
  272.4 3.9 collective-permute-start.1
  276.4 6.4 convolution_convert_fusion.14
  285.4 3.4 convolution_convert_fusion.15
  288.8 3.4 convolution_convert_fusion.9
  292.3 5.7 convolution_convert_fusion.10
  298.0 7.1 convolution_convert_fusion.16
  305.1 4.9 convolution_convert_fusion.11
  310.0 7.2 convolution_convert_fusion.7
  321.3 4.5 convolution_convert_fusion.12
  330.9 3.4 collective-permute-start.3
  336.7 3.1 fusion.16
  339.8 56.6 %reduce-scatter.5.cloned.1.call-done = bf16[256,2048]{1,0:T(8,128)(2,1)} async-done(((bf16[2048,2048]{1,0:T(8,128)(2,1)}), bf16[256,2048]{1,0:T(8,128)(2,1)}) %reduce-scatter.5.cloned.1.call-update) | async-done | bytes 1048592 | tf_op jit(solution)/shard_map/reduce_scatter | solution.py:249
  396.4 4.6 fusion.13
  403.2 4.1 all-to-all-start
  407.4 7.2 convolution_convert_fusion.8
  414.5 3.0 add.213
  419.2 6.1 collective-permute-start.7
  429.4 2.9 add.226
  437.2 2.9 add.215
  440.1 4.3 convolution_convert_fusion.3
  459.9 6.9 convolution_convert_fusion
  468.0 6.6 convolution_convert_fusion.17
  481.1 11.3 %collective-permute-start.6 = (bf16[256,2048]{1,0:T(8,128)(2,1)S(1)}, bf16[256,2048]{1,0:T(8,128)(2,1)S(1)}, u32[]{:S(2)}, u32[]{:S(2)}) collective-permute-start(bf16[256,2048]{1,0:T(8,128)(2,1)S(1)} %copy-done.22), channel_id=1, source_target_pairs={{0,1},{3,2},{4,5},{7,6},{8,9},{11,10},{12,13},{15,14},{16,17},{19,... | collective-permute-start | bytes 3145736 | tf_op jit(solution)/shard_map/ppermute | solution.py:188
  493.8 4.9 convolution_convert_fusion.6
  498.7 3.9 collective-permute-start.10
  507.3 8.6 %collective-permute-done.6 = bf16[256,2048]{1,0:T(8,128)(2,1)S(1)} collective-permute-done((bf16[256,2048]{1,0:T(8,128)(2,1)S(1)}, bf16[256,2048]{1,0:T(8,128)(2,1)S(1)}, u32[]{:S(2)}, u32[]{:S(2)}) %collective-permute-start.6) | collective-permute-done | bytes 1048608 | tf_op jit(solution)/shard_map/ppermute | solution.py:188
  519.3 19.1 %collective-permute-done.5 = bf16[256,2048]{1,0:T(8,128)(2,1)S(1)} collective-permute-done((bf16[256,2048]{1,0:T(8,128)(2,1)S(1)}, bf16[256,2048]{1,0:T(8,128)(2,1)S(1)}, u32[]{:S(2)}, u32[]{:S(2)}) %collective-permute-start.5) | collective-permute-done | bytes 1048608 | tf_op jit(solution)/shard_map/ppermute | solution.py:188
  540.8 17.9 %collective-permute-done.10 = bf16[256,2048]{1,0:T(8,128)(2,1)S(1)} collective-permute-done((bf16[256,2048]{1,0:T(8,128)(2,1)S(1)}, bf16[256,2048]{1,0:T(8,128)(2,1)S(1)}, u32[]{:S(2)}, u32[]{:S(2)}) %collective-permute-start.10) | collective-permute-done | bytes 1048608 | tf_op jit(solution)/shard_map/ppermute | solution.py:188
  560.8 8.6 %collective-permute-done.37 = bf16[256,2048]{1,0:T(8,128)(2,1)S(1)} collective-permute-done((bf16[256,2048]{1,0:T(8,128)(2,1)S(1)}, bf16[256,2048]{1,0:T(8,128)(2,1)S(1)}, u32[]{:S(2)}, u32[]{:S(2)}) %collective-permute-start.37) | collective-permute-done | bytes 1048608 | tf_op jit(solution)/shard_map/ppermute | solution.py:188
  570.9 18.8 %collective-permute-done.36 = bf16[256,2048]{1,0:T(8,128)(2,1)S(1)} collective-permute-done((bf16[256,2048]{1,0:T(8,128)(2,1)S(1)}, bf16[256,2048]{1,0:T(8,128)(2,1)S(1)}, u32[]{:S(2)}, u32[]{:S(2)}) %collective-permute-start.36) | collective-permute-done | bytes 1048608 | tf_op jit(solution)/shard_map/ppermute | solution.py:188
  599.8 14.9 %collective-permute-done.8 = bf16[256,2048]{1,0:T(8,128)(2,1)S(1)} collective-permute-done((bf16[256,2048]{1,0:T(8,128)(2,1)S(1)}, bf16[256,2048]{1,0:T(8,128)(2,1)S(1)}, u32[]{:S(2)}, u32[]{:S(2)}) %collective-permute-start.8) | collective-permute-done | bytes 1048608 | tf_op jit(solution)/shard_map/ppermute | solution.py:188
  615.9 18.7 %collective-permute-done.13 = bf16[256,2048]{1,0:T(8,128)(2,1)S(1)} collective-permute-done((bf16[256,2048]{1,0:T(8,128)(2,1)S(1)}, bf16[256,2048]{1,0:T(8,128)(2,1)S(1)}, u32[]{:S(2)}, u32[]{:S(2)}) %collective-permute-start.13) | collective-permute-done | bytes 1048608 | tf_op jit(solution)/shard_map/ppermute | solution.py:188
  635.8 4.6 maximum_convert_fusion
  642.5 6.4 convolution_convert_fusion.4
  648.9 9.9 %collective-permute-start.11 = (bf16[2048,384]{1,0:T(8,128)(2,1)}, bf16[2048,384]{1,0:T(8,128)(2,1)}, u32[]{:S(2)}, u32[]{:S(2)}) collective-permute-start(bf16[2048,384]{1,0:T(8,128)(2,1)} %convolution_convert_fusion.4), channel_id=1, source_target_pairs={{0,1},{3,2},{4,5},{7,6},{8,9},{11,10},{12,13},{15,14},{16,17},{19,... | collective-permute-start | bytes 4718600 | tf_op jit(solution)/shard_map/ppermute | solution.py:188
  669.7 20.0 %collective-permute-start.12 = (bf16[128,2048]{1,0:T(8,128)(2,1)}, bf16[128,2048]{1,0:T(8,128)(2,1)S(1)}, u32[]{:S(2)}, u32[]{:S(2)}) collective-permute-start(bf16[128,2048]{1,0:T(8,128)(2,1)} %reduce-scatter.11.cloned.1.call-done), channel_id=1, source_target_pairs={{0,1},{3,2},{4,5},{7,6},{8,9},{11,10},{12,13},{15,14},{16,17},{19,... | collective-permute-start | bytes 1572872 | tf_op jit(solution)/shard_map/ppermute | solution.py:188
  692.3 7.6 collective-permute-done.12
  704.2 2.6 constant_dynamic-update-slice_fusion.7
  706.8 5.6 collective-permute-done.31
  712.4 2.6 constant_dynamic-update-slice_fusion.6
  715.0 15.4 %collective-permute-done.30 = bf16[256,2048]{1,0:T(8,128)(2,1)} collective-permute-done((bf16[256,2048]{1,0:T(8,128)(2,1)}, bf16[256,2048]{1,0:T(8,128)(2,1)}, u32[]{:S(2)}, u32[]{:S(2)}) %collective-permute-start.30) | collective-permute-done | bytes 1048608 | tf_op jit(solution)/shard_map/ppermute | solution.py:188
  731.1 2.6 constant_dynamic-update-slice_fusion.5
  738.0 11.8 %fusion.109 = (f32[2048,1024]{1,0:T(8,128)}, f32[2048,1024]{1,0:T(8,128)}) fusion(bf16[2048,2048]{1,0:T(8,128)(2,1)} %constant_dynamic-update-slice_fusion.5), kind=kLoop, calls=%fused_computation.215 | loop fusion | bytes 33554432 | tf_op jit(solution)/shard_map/slice | solution.py:332
  750.4 17.0 %collective-permute-done.29 = bf16[128,2048]{1,0:T(8,128)(2,1)S(1)} collective-permute-done((bf16[128,2048]{1,0:T(8,128)(2,1)S(1)}, bf16[128,2048]{1,0:T(8,128)(2,1)S(1)}, u32[]{:S(2)}, u32[]{:S(2)}) %collective-permute-start.29) | collective-permute-done | bytes 524320 | tf_op jit(solution)/shard_map/ppermute | solution.py:188
  768.5 29.1 %collective-permute-done.28 = bf16[2048,384]{1,0:T(8,128)(2,1)} collective-permute-done((bf16[2048,384]{1,0:T(8,128)(2,1)}, bf16[2048,384]{1,0:T(8,128)(2,1)}, u32[]{:S(2)}, u32[]{:S(2)}) %collective-permute-start.28) | collective-permute-done | bytes 1572896 | tf_op jit(solution)/shard_map/ppermute | solution.py:188
  802.8 17.7 %psum.14 = f32[4104]{0:T(1024)S(1)} all-reduce(f32[4104]{0:T(1024)S(1)} %pad_maximum_fusion.6), channel_id=1, replica_groups=mesh['heads'=8,'batch'=4] {'batch'}, use_global_device_ids=true, to_apply=%region_23.24 | all-reduce | flops 4104 | bytes 32832 | tf_op jit(solution)/shard_map/psum | solution.py:317
  820.5 22.3 %psum.15 = f32[4104]{0:T(1024)S(1)} all-reduce(f32[4104]{0:T(1024)S(1)} %psum.14), channel_id=1, replica_groups=mesh['heads'=8,'batch'=4] {'heads'}, use_global_device_ids=true, to_apply=%region_24.25 | all-reduce | flops 4104 | bytes 32832 | tf_op jit(solution)/shard_map/psum | solution.py:316
  844.0 3.3 fusion.11
  (345 shorter events, 136.8 us)
Async XLA Ops:
  7.2 59.8 %all-gather.5.cloned.1.call-start = ((), (), s32[]{:S(2)}) async-start(), calls=%async_computation.5 | async-start | bytes 9437184 | tf_op jit(solution)/shard_map/all_gather | solution.py:246
  7.9 97.7 %all-gather.9.cloned.1.call-start = ((), (), s32[]{:S(2)}) async-start(), calls=%async_computation.7 | async-start | bytes 4718592 | tf_op jit(solution)/shard_map/all_gather | solution.py:246
  8.7 136.9 %all-gather.7.cloned.1.call-start = ((), (), s32[]{:S(2)}) async-start(), calls=%async_computation.6 | async-start | bytes 4718592 | tf_op jit(solution)/shard_map/all_gather | solution.py:271
  10.8 71.9 %copy-start.56 = (s32[2,512]{1,0:T(2,128)}, s32[2,512]{1,0:T(2,128)S(1)}, u32[]{:S(2)}) copy-start(s32[2,512]{1,0:T(2,128)S(1)} %get-tuple-element.266) | copy-start | bytes 12292
  10.8 74.2 %copy-start.54 = (s32[2,512]{1,0:T(2,128)}, s32[2,512]{1,0:T(2,128)S(1)}, u32[]{:S(2)}) copy-start(s32[2,512]{1,0:T(2,128)S(1)} %get-tuple-element.265) | copy-start | bytes 12292
  13.5 69.2 %copy-start.58 = (pred[2,512]{1,0:T(4,128)(4,1)}, pred[2,512]{1,0:T(4,128)(4,1)S(1)}, u32[]{:S(2)}) copy-start(pred[2,512]{1,0:T(4,128)(4,1)S(1)} %get-tuple-element.268) | copy-start | bytes 3076
  14.7 57.6 %copy-start.37 = (bf16[2048,384]{1,0:T(8,128)(2,1)}, bf16[2048,384]{1,0:T(8,128)(2,1)S(1)}, u32[]{:S(2)}) copy-start(bf16[2048,384]{1,0:T(8,128)(2,1)S(1)} %constant_dynamic-update-slice_fusion) | copy-start | bytes 4718596
  16.1 56.1 %copy-start.41 = (f32[2048]{0:T(1024)S(1)}, f32[2048]{0:T(1024)}, u32[]{:S(2)}) copy-start(f32[2048]{0:T(1024)} %param.25) | copy-start | bytes 24580
  92.6 109.2 %all-gather.11.cloned.1.call-start = ((), (), s32[]{:S(2)}) async-start(), calls=%async_computation.9 | async-start | bytes 9437184 | tf_op jit(solution)/shard_map/all_gather | solution.py:246
  93.1 243.5 %reduce-scatter.7.cloned.1.call-start = ((), (), s32[]{:S(2)}) async-start(), calls=%async_computation.10 | async-start | bytes 9437184 | tf_op jit(solution)/shard_map/reduce_scatter | solution.py:249
  100.5 64.5 %copy-start.39 = (f32[2048]{0:T(1024)S(1)}, f32[2048]{0:T(1024)}, u32[]{:S(2)}) copy-start(f32[2048]{0:T(1024)} %param.26) | copy-start | bytes 24580
  249.4 147.0 %reduce-scatter.5.cloned.1.call-start = ((), (), s32[]{:S(2)}) async-start(), calls=%async_computation.8 | async-start | bytes 9437184 | tf_op jit(solution)/shard_map/reduce_scatter | solution.py:249
  266.2 19.2 %slice-start.2 = ((s8[8388608]{0:T(1024)(128)(4,1)}), s8[4194304]{0:T(1024)(128)(4,1)S(1)}, s32[]{:S(2)}) async-start(s8[8388608]{0:T(1024)(128)(4,1)} %bitcast.109), calls=%async_computation.15 | async-start | bytes 8388608
  272.4 13.0 %slice-start.3 = ((s8[8388608]{0:T(1024)(128)(4,1)}), s8[4194304]{0:T(1024)(128)(4,1)S(1)}, s32[]{:S(2)}) async-start(s8[8388608]{0:T(1024)(128)(4,1)} %bitcast.109), calls=%async_computation.16 | async-start | bytes 8388608
  272.4 53.4 %collective-permute-start.1 = (bf16[256,2048]{1,0:T(8,128)(2,1)S(1)}, bf16[256,2048]{1,0:T(8,128)(2,1)S(1)}, u32[]{:S(2)}, u32[]{:S(2)}) collective-permute-start(bf16[256,2048]{1,0:T(8,128)(2,1)S(1)} %convolution_convert_fusion.13), channel_id=1, source_target_pairs={{0,1},{3,2},{4,5},{7,6},{8,9},{11,10},{12,13},{15,14},{16,17},{19,... | collective-permute-start | bytes 3145736 | tf_op jit(solution)/shard_map/ppermute | solution.py:188
  282.8 45.2 %collective-permute-start = (bf16[256,2048]{1,0:T(8,128)(2,1)S(1)}, bf16[256,2048]{1,0:T(8,128)(2,1)S(1)}, u32[]{:S(2)}, u32[]{:S(2)}) collective-permute-start(bf16[256,2048]{1,0:T(8,128)(2,1)S(1)} %convolution_convert_fusion.14), channel_id=1, source_target_pairs={{0,1},{3,2},{4,5},{7,6},{8,9},{11,10},{12,13},{15,14},{16,17},{19,... | collective-permute-start | bytes 3145736 | tf_op jit(solution)/shard_map/ppermute | solution.py:188
  317.2 97.4 %collective-permute-start.4 = (bf16[256,2048]{1,0:T(8,128)(2,1)}, bf16[256,2048]{1,0:T(8,128)(2,1)}, u32[]{:S(2)}, u32[]{:S(2)}) collective-permute-start(bf16[256,2048]{1,0:T(8,128)(2,1)} %convolution_convert_fusion.11), channel_id=1, source_target_pairs={{0,1},{3,2},{4,5},{7,6},{8,9},{11,10},{12,13},{15,14},{16,17},{19,... | collective-permute-start | bytes 3145736 | tf_op jit(solution)/shard_map/ppermute | solution.py:188
  326.3 92.9 %collective-permute-start.27 = (bf16[256,2048]{1,0:T(8,128)(2,1)S(1)}, bf16[256,2048]{1,0:T(8,128)(2,1)}, u32[]{:S(2)}, u32[]{:S(2)}) collective-permute-start(bf16[256,2048]{1,0:T(8,128)(2,1)S(1)} %add.211), channel_id=1, source_target_pairs={{1,2},{2,1},{5,6},{6,5},{9,10},{10,9},{13,14},{14,13},{17,18},{18,... | collective-permute-start | bytes 3145736 | tf_op jit(solution)/shard_map/ppermute | solution.py:188
  329.3 98.6 %collective-permute-start.26 = (bf16[256,2048]{1,0:T(8,128)(2,1)}, bf16[256,2048]{1,0:T(8,128)(2,1)}, u32[]{:S(2)}, u32[]{:S(2)}) collective-permute-start(bf16[256,2048]{1,0:T(8,128)(2,1)} %add.212), channel_id=1, source_target_pairs={{1,2},{2,1},{5,6},{6,5},{9,10},{10,9},{13,14},{14,13},{17,18},{18,... | collective-permute-start | bytes 3145736 | tf_op jit(solution)/shard_map/ppermute | solution.py:188
  330.9 101.4 %collective-permute-start.3 = (bf16[256,2048]{1,0:T(8,128)(2,1)}, bf16[256,2048]{1,0:T(8,128)(2,1)}, u32[]{:S(2)}, u32[]{:S(2)}) collective-permute-start(bf16[256,2048]{1,0:T(8,128)(2,1)} %convolution_convert_fusion.12), channel_id=1, source_target_pairs={{0,1},{3,2},{4,5},{7,6},{8,9},{11,10},{12,13},{15,14},{16,17},{19,... | collective-permute-start | bytes 3145736 | tf_op jit(solution)/shard_map/ppermute | solution.py:188
  334.4 101.2 %collective-permute-start.2 = (bf16[256,2048]{1,0:T(8,128)(2,1)}, bf16[256,2048]{1,0:T(8,128)(2,1)}, u32[]{:S(2)}, u32[]{:S(2)}) collective-permute-start(bf16[256,2048]{1,0:T(8,128)(2,1)} %convolution_convert_fusion.15), channel_id=1, source_target_pairs={{0,1},{3,2},{4,5},{7,6},{8,9},{11,10},{12,13},{15,14},{16,17},{19,... | collective-permute-start | bytes 3145736 | tf_op jit(solution)/shard_map/ppermute | solution.py:188
  403.2 41.4 %all-to-all-start = ((bf16[256,8,128]{2,0,1:T(8,128)(2,1)}), bf16[256,8,128]{2,0,1:T(8,128)(2,1)}, u32[]{:S(2)}, u32[]{:S(2)}) async-start(bf16[256,8,128]{2,0,1:T(8,128)(2,1)} %bitcast.119), calls=%async_computation.2 | async-start | bytes 1048576 | tf_op jit(solution)/shard_map/all_to_all | solution.py:304
  407.3 262.3 %reduce-scatter.11.cloned.1.call-start = ((), (), s32[]{:S(2)}) async-start(), calls=%async_computation.12 | async-start | bytes 4718592 | tf_op jit(solution)/shard_map/reduce_scatter | solution.py:249
  417.5 49.3 %collective-permute-start.25 = (bf16[256,2048]{1,0:T(8,128)(2,1)}, bf16[256,2048]{1,0:T(8,128)(2,1)}, u32[]{:S(2)}, u32[]{:S(2)}) collective-permute-start(bf16[256,2048]{1,0:T(8,128)(2,1)} %add.213), channel_id=1, source_target_pairs={{1,2},{2,1},{5,6},{6,5},{9,10},{10,9},{13,14},{14,13},{17,18},{18,... | collective-permute-start | bytes 3145736 | tf_op jit(solution)/shard_map/ppermute | solution.py:188
  419.2 57.6 %collective-permute-start.7 = (bf16[256,2048]{1,0:T(8,128)(2,1)}, bf16[256,2048]{1,0:T(8,128)(2,1)}, u32[]{:S(2)}, u32[]{:S(2)}) collective-permute-start(bf16[256,2048]{1,0:T(8,128)(2,1)} %convolution_convert_fusion.9), channel_id=1, source_target_pairs={{0,1},{3,2},{4,5},{7,6},{8,9},{11,10},{12,13},{15,14},{16,17},{19,... | collective-permute-start | bytes 3145736 | tf_op jit(solution)/shard_map/ppermute | solution.py:188
  427.9 52.2 %collective-permute-start.41 = (bf16[256,2048]{1,0:T(8,128)(2,1)}, bf16[256,2048]{1,0:T(8,128)(2,1)}, u32[]{:S(2)}, u32[]{:S(2)}) collective-permute-start(bf16[256,2048]{1,0:T(8,128)(2,1)} %add.225), channel_id=1, source_target_pairs={{1,0},{2,3},{5,4},{6,7},{9,8},{10,11},{13,12},{14,15},{17,16},{18,... | collective-permute-start | bytes 3145736 | tf_op jit(solution)/shard_map/ppermute | solution.py:188
  432.3 48.7 %collective-permute-start.40 = (bf16[256,2048]{1,0:T(8,128)(2,1)}, bf16[256,2048]{1,0:T(8,128)(2,1)}, u32[]{:S(2)}, u32[]{:S(2)}) collective-permute-start(bf16[256,2048]{1,0:T(8,128)(2,1)} %add.226), channel_id=1, source_target_pairs={{1,0},{2,3},{5,4},{6,7},{9,8},{10,11},{13,12},{14,15},{17,16},{18,... | collective-permute-start | bytes 3145736 | tf_op jit(solution)/shard_map/ppermute | solution.py:188
  435.6 56.8 %collective-permute-start.24 = (bf16[256,2048]{1,0:T(8,128)(2,1)S(1)}, bf16[256,2048]{1,0:T(8,128)(2,1)}, u32[]{:S(2)}, u32[]{:S(2)}) collective-permute-start(bf16[256,2048]{1,0:T(8,128)(2,1)S(1)} %add.214), channel_id=1, source_target_pairs={{1,2},{2,1},{5,6},{6,5},{9,10},{10,9},{13,14},{14,13},{17,18},{18,... | collective-permute-start | bytes 3145736 | tf_op jit(solution)/shard_map/ppermute | solution.py:188
  444.6 356.3 %reduce-scatter.9.cloned.1.call-start = ((), (), s32[]{:S(2)}) async-start(), calls=%async_computation.11 | async-start | bytes 9437184 | tf_op jit(solution)/shard_map/reduce_scatter | solution.py:249
  466.9 31.8 %collective-permute-start.23 = (bf16[256,2048]{1,0:T(8,128)(2,1)}, bf16[256,2048]{1,0:T(8,128)(2,1)S(1)}, u32[]{:S(2)}, u32[]{:S(2)}) collective-permute-start(bf16[256,2048]{1,0:T(8,128)(2,1)} %add.215), channel_id=1, source_target_pairs={{1,2},{2,1},{5,6},{6,5},{9,10},{10,9},{13,14},{14,13},{17,18},{18,... | collective-permute-start | bytes 3145736 | tf_op jit(solution)/shard_map/ppermute | solution.py:188
  474.7 17.7 %copy-start.21 = (bf16[256,2048]{1,0:T(8,128)(2,1)S(1)}, bf16[256,2048]{1,0:T(8,128)(2,1)}, u32[]{:S(2)}) copy-start(bf16[256,2048]{1,0:T(8,128)(2,1)} %convolution_convert_fusion.16) | copy-start | bytes 3145732
  474.7 19.1 %copy-start.65 = (bf16[2048,1024]{0,1:T(8,128)(2,1)S(1)}, bf16[2048,1024]{0,1:T(8,128)(2,1)}, u32[]{:S(2)}) copy-start(bf16[2048,1024]{0,1:T(8,128)(2,1)} %copy-done.63) | copy-start | bytes 12582916
  476.8 41.2 %collective-permute-start.39 = (bf16[256,2048]{1,0:T(8,128)(2,1)S(1)}, bf16[256,2048]{1,0:T(8,128)(2,1)S(1)}, u32[]{:S(2)}, u32[]{:S(2)}) collective-permute-start(bf16[256,2048]{1,0:T(8,128)(2,1)S(1)} %add.227), channel_id=1, source_target_pairs={{1,0},{2,3},{5,4},{6,7},{9,8},{10,11},{13,12},{14,15},{17,16},{18,... | collective-permute-start | bytes 3145736 | tf_op jit(solution)/shard_map/ppermute | solution.py:188
  480.1 18.6 %copy-start.19 = (bf16[256,2048]{1,0:T(8,128)(2,1)S(1)}, bf16[256,2048]{1,0:T(8,128)(2,1)}, u32[]{:S(2)}) copy-start(bf16[256,2048]{1,0:T(8,128)(2,1)} %convolution_convert_fusion.7) | copy-start | bytes 3145732
  480.2 25.8 %collective-permute-start.22 = (bf16[256,2048]{1,0:T(8,128)(2,1)S(1)}, bf16[256,2048]{1,0:T(8,128)(2,1)S(1)}, u32[]{:S(2)}, u32[]{:S(2)}) collective-permute-start(bf16[256,2048]{1,0:T(8,128)(2,1)S(1)} %add.216), channel_id=1, source_target_pairs={{1,2},{2,1},{5,6},{6,5},{9,10},{10,9},{13,14},{14,13},{17,18},{18,... | collective-permute-start | bytes 3145736 | tf_op jit(solution)/shard_map/ppermute | solution.py:188
  481.1 34.8 %collective-permute-start.6 = (bf16[256,2048]{1,0:T(8,128)(2,1)S(1)}, bf16[256,2048]{1,0:T(8,128)(2,1)S(1)}, u32[]{:S(2)}, u32[]{:S(2)}) collective-permute-start(bf16[256,2048]{1,0:T(8,128)(2,1)S(1)} %copy-done.22), channel_id=1, source_target_pairs={{0,1},{3,2},{4,5},{7,6},{8,9},{11,10},{12,13},{15,14},{16,17},{19,... | collective-permute-start | bytes 3145736 | tf_op jit(solution)/shard_map/ppermute | solution.py:188
  492.4 46.0 %collective-permute-start.5 = (bf16[256,2048]{1,0:T(8,128)(2,1)S(1)}, bf16[256,2048]{1,0:T(8,128)(2,1)S(1)}, u32[]{:S(2)}, u32[]{:S(2)}) collective-permute-start(bf16[256,2048]{1,0:T(8,128)(2,1)S(1)} %copy-done.21), channel_id=1, source_target_pairs={{0,1},{3,2},{4,5},{7,6},{8,9},{11,10},{12,13},{15,14},{16,17},{19,... | collective-permute-start | bytes 3145736 | tf_op jit(solution)/shard_map/ppermute | solution.py:188
  498.7 60.0 %collective-permute-start.10 = (bf16[256,2048]{1,0:T(8,128)(2,1)S(1)}, bf16[256,2048]{1,0:T(8,128)(2,1)S(1)}, u32[]{:S(2)}, u32[]{:S(2)}) collective-permute-start(bf16[256,2048]{1,0:T(8,128)(2,1)S(1)} %copy-done.19), channel_id=1, source_target_pairs={{0,1},{3,2},{4,5},{7,6},{8,9},{11,10},{12,13},{15,14},{16,17},{19,... | collective-permute-start | bytes 3145736 | tf_op jit(solution)/shard_map/ppermute | solution.py:188
  506.0 54.0 %collective-permute-start.38 = (bf16[256,2048]{1,0:T(8,128)(2,1)S(1)}, bf16[256,2048]{1,0:T(8,128)(2,1)S(1)}, u32[]{:S(2)}, u32[]{:S(2)}) collective-permute-start(bf16[256,2048]{1,0:T(8,128)(2,1)S(1)} %add.228), channel_id=1, source_target_pairs={{1,0},{2,3},{5,4},{6,7},{9,8},{10,11},{13,12},{14,15},{17,16},{18,... | collective-permute-start | bytes 3145736 | tf_op jit(solution)/shard_map/ppermute | solution.py:188
  515.9 53.5 %collective-permute-start.37 = (bf16[256,2048]{1,0:T(8,128)(2,1)S(1)}, bf16[256,2048]{1,0:T(8,128)(2,1)S(1)}, u32[]{:S(2)}, u32[]{:S(2)}) collective-permute-start(bf16[256,2048]{1,0:T(8,128)(2,1)S(1)} %add.229), channel_id=1, source_target_pairs={{1,0},{2,3},{5,4},{6,7},{9,8},{10,11},{13,12},{14,15},{17,16},{18,... | collective-permute-start | bytes 3145736 | tf_op jit(solution)/shard_map/ppermute | solution.py:188
  518.0 71.7 %collective-permute-start.36 = (bf16[256,2048]{1,0:T(8,128)(2,1)S(1)}, bf16[256,2048]{1,0:T(8,128)(2,1)S(1)}, u32[]{:S(2)}, u32[]{:S(2)}) collective-permute-start(bf16[256,2048]{1,0:T(8,128)(2,1)S(1)} %add.230), channel_id=1, source_target_pairs={{1,0},{2,3},{5,4},{6,7},{9,8},{10,11},{13,12},{14,15},{17,16},{18,... | collective-permute-start | bytes 3145736 | tf_op jit(solution)/shard_map/ppermute | solution.py:188
  538.4 52.8 %collective-permute-start.21 = (bf16[256,2048]{1,0:T(8,128)(2,1)S(1)}, bf16[256,2048]{1,0:T(8,128)(2,1)S(1)}, u32[]{:S(2)}, u32[]{:S(2)}) collective-permute-start(bf16[256,2048]{1,0:T(8,128)(2,1)S(1)} %add.217), channel_id=1, source_target_pairs={{1,2},{2,1},{5,6},{6,5},{9,10},{10,9},{13,14},{14,13},{17,18},{18,... | collective-permute-start | bytes 3145736 | tf_op jit(solution)/shard_map/ppermute | solution.py:188
  540.4 29.0 %copy-start.20 = (bf16[256,2048]{1,0:T(8,128)(2,1)S(1)}, bf16[256,2048]{1,0:T(8,128)(2,1)}, u32[]{:S(2)}) copy-start(bf16[256,2048]{1,0:T(8,128)(2,1)} %convolution_convert_fusion.8) | copy-start | bytes 3145732
  558.8 34.4 %collective-permute-start.20 = (bf16[256,2048]{1,0:T(8,128)(2,1)S(1)}, bf16[256,2048]{1,0:T(8,128)(2,1)S(1)}, u32[]{:S(2)}, u32[]{:S(2)}) collective-permute-start(bf16[256,2048]{1,0:T(8,128)(2,1)S(1)} %add.218), channel_id=1, source_target_pairs={{1,2},{2,1},{5,6},{6,5},{9,10},{10,9},{13,14},{14,13},{17,18},{18,... | collective-permute-start | bytes 3145736 | tf_op jit(solution)/shard_map/ppermute | solution.py:188
  560.0 36.4 %collective-permute-start.19 = (bf16[256,2048]{1,0:T(8,128)(2,1)S(1)}, bf16[256,2048]{1,0:T(8,128)(2,1)S(1)}, u32[]{:S(2)}, u32[]{:S(2)}) collective-permute-start(bf16[256,2048]{1,0:T(8,128)(2,1)S(1)} %add.219), channel_id=1, source_target_pairs={{1,2},{2,1},{5,6},{6,5},{9,10},{10,9},{13,14},{14,13},{17,18},{18,... | collective-permute-start | bytes 3145736 | tf_op jit(solution)/shard_map/ppermute | solution.py:188
  569.4 28.7 %collective-permute-start.9 = (bf16[256,2048]{1,0:T(8,128)(2,1)S(1)}, bf16[256,2048]{1,0:T(8,128)(2,1)S(1)}, u32[]{:S(2)}, u32[]{:S(2)}) collective-permute-start(bf16[256,2048]{1,0:T(8,128)(2,1)S(1)} %copy-done.20), channel_id=1, source_target_pairs={{0,1},{3,2},{4,5},{7,6},{8,9},{11,10},{12,13},{15,14},{16,17},{19,... | collective-permute-start | bytes 3145736 | tf_op jit(solution)/shard_map/ppermute | solution.py:188
  589.7 25.0 %collective-permute-start.8 = (bf16[256,2048]{1,0:T(8,128)(2,1)S(1)}, bf16[256,2048]{1,0:T(8,128)(2,1)S(1)}, u32[]{:S(2)}, u32[]{:S(2)}) collective-permute-start(bf16[256,2048]{1,0:T(8,128)(2,1)S(1)} %convolution_convert_fusion.17), channel_id=1, source_target_pairs={{0,1},{3,2},{4,5},{7,6},{8,9},{11,10},{12,13},{15,14},{16,17},{19,... | collective-permute-start | bytes 3145736 | tf_op jit(solution)/shard_map/ppermute | solution.py:188
  591.2 43.3 %collective-permute-start.13 = (bf16[256,2048]{1,0:T(8,128)(2,1)S(1)}, bf16[256,2048]{1,0:T(8,128)(2,1)S(1)}, u32[]{:S(2)}, u32[]{:S(2)}) collective-permute-start(bf16[256,2048]{1,0:T(8,128)(2,1)S(1)} %convolution_convert_fusion.6), channel_id=1, source_target_pairs={{0,1},{3,2},{4,5},{7,6},{8,9},{11,10},{12,13},{15,14},{16,17},{19,... | collective-permute-start | bytes 3145736 | tf_op jit(solution)/shard_map/ppermute | solution.py:188
  593.1 48.6 %collective-permute-start.35 = (bf16[256,2048]{1,0:T(8,128)(2,1)S(1)}, bf16[256,2048]{1,0:T(8,128)(2,1)S(1)}, u32[]{:S(2)}, u32[]{:S(2)}) collective-permute-start(bf16[256,2048]{1,0:T(8,128)(2,1)S(1)} %add.231), channel_id=1, source_target_pairs={{1,0},{2,3},{5,4},{6,7},{9,8},{10,11},{13,12},{14,15},{17,16},{18,... | collective-permute-start | bytes 3145736 | tf_op jit(solution)/shard_map/ppermute | solution.py:188
  596.4 52.5 %collective-permute-start.34 = (bf16[256,2048]{1,0:T(8,128)(2,1)S(1)}, bf16[256,2048]{1,0:T(8,128)(2,1)S(1)}, u32[]{:S(2)}, u32[]{:S(2)}) collective-permute-start(bf16[256,2048]{1,0:T(8,128)(2,1)S(1)} %add.232), channel_id=1, source_target_pairs={{1,0},{2,3},{5,4},{6,7},{9,8},{10,11},{13,12},{14,15},{17,16},{18,... | collective-permute-start | bytes 3145736 | tf_op jit(solution)/shard_map/ppermute | solution.py:188
  598.1 66.2 %collective-permute-start.33 = (bf16[256,2048]{1,0:T(8,128)(2,1)S(1)}, bf16[256,2048]{1,0:T(8,128)(2,1)S(1)}, u32[]{:S(2)}, u32[]{:S(2)}) collective-permute-start(bf16[256,2048]{1,0:T(8,128)(2,1)S(1)} %add.233), channel_id=1, source_target_pairs={{1,0},{2,3},{5,4},{6,7},{9,8},{10,11},{13,12},{14,15},{17,16},{18,... | collective-permute-start | bytes 3145736 | tf_op jit(solution)/shard_map/ppermute | solution.py:188
  614.7 45.5 %collective-permute-start.18 = (bf16[256,2048]{1,0:T(8,128)(2,1)S(1)}, bf16[256,2048]{1,0:T(8,128)(2,1)S(1)}, u32[]{:S(2)}, u32[]{:S(2)}) collective-permute-start(bf16[256,2048]{1,0:T(8,128)(2,1)S(1)} %add.220), channel_id=1, source_target_pairs={{1,2},{2,1},{5,6},{6,5},{9,10},{10,9},{13,14},{14,13},{17,18},{18,... | collective-permute-start | bytes 3145736 | tf_op jit(solution)/shard_map/ppermute | solution.py:188
  615.5 27.0 %slice-start = ((s8[8388608]{0:T(1024)(128)(4,1)}), s8[4194304]{0:T(1024)(128)(4,1)S(1)}, s32[]{:S(2)}) async-start(s8[8388608]{0:T(1024)(128)(4,1)} %bitcast.107), calls=%async_computation.13 | async-start | bytes 8388608
  634.5 29.8 %collective-permute-start.17 = (bf16[256,2048]{1,0:T(8,128)(2,1)S(1)}, bf16[256,2048]{1,0:T(8,128)(2,1)S(1)}, u32[]{:S(2)}, u32[]{:S(2)}) collective-permute-start(bf16[256,2048]{1,0:T(8,128)(2,1)S(1)} %add.221), channel_id=1, source_target_pairs={{1,2},{2,1},{5,6},{6,5},{9,10},{10,9},{13,14},{14,13},{17,18},{18,... | collective-permute-start | bytes 3145736 | tf_op jit(solution)/shard_map/ppermute | solution.py:188
  641.7 25.3 %collective-permute-start.16 = (bf16[256,2048]{1,0:T(8,128)(2,1)S(1)}, bf16[256,2048]{1,0:T(8,128)(2,1)S(1)}, u32[]{:S(2)}, u32[]{:S(2)}) collective-permute-start(bf16[256,2048]{1,0:T(8,128)(2,1)S(1)} %add.222), channel_id=1, source_target_pairs={{1,2},{2,1},{5,6},{6,5},{9,10},{10,9},{13,14},{14,13},{17,18},{18,... | collective-permute-start | bytes 3145736 | tf_op jit(solution)/shard_map/ppermute | solution.py:188
  648.9 52.2 %collective-permute-start.11 = (bf16[2048,384]{1,0:T(8,128)(2,1)}, bf16[2048,384]{1,0:T(8,128)(2,1)}, u32[]{:S(2)}, u32[]{:S(2)}) collective-permute-start(bf16[2048,384]{1,0:T(8,128)(2,1)} %convolution_convert_fusion.4), channel_id=1, source_target_pairs={{0,1},{3,2},{4,5},{7,6},{8,9},{11,10},{12,13},{15,14},{16,17},{19,... | collective-permute-start | bytes 4718600 | tf_op jit(solution)/shard_map/ppermute | solution.py:188
  661.6 30.7 %collective-permute-start.32 = (bf16[256,2048]{1,0:T(8,128)(2,1)}, bf16[256,2048]{1,0:T(8,128)(2,1)}, u32[]{:S(2)}, u32[]{:S(2)}) collective-permute-start(bf16[256,2048]{1,0:T(8,128)(2,1)} %add.234), channel_id=1, source_target_pairs={{1,0},{2,3},{5,4},{6,7},{9,8},{10,11},{13,12},{14,15},{17,16},{18,... | collective-permute-start | bytes 3145736 | tf_op jit(solution)/shard_map/ppermute | solution.py:188
  665.7 46.7 %collective-permute-start.31 = (bf16[256,2048]{1,0:T(8,128)(2,1)}, bf16[256,2048]{1,0:T(8,128)(2,1)}, u32[]{:S(2)}, u32[]{:S(2)}) collective-permute-start(bf16[256,2048]{1,0:T(8,128)(2,1)} %add.235), channel_id=1, source_target_pairs={{1,0},{2,3},{5,4},{6,7},{9,8},{10,11},{13,12},{14,15},{17,16},{18,... | collective-permute-start | bytes 3145736 | tf_op jit(solution)/shard_map/ppermute | solution.py:188
  668.4 62.1 %collective-permute-start.30 = (bf16[256,2048]{1,0:T(8,128)(2,1)}, bf16[256,2048]{1,0:T(8,128)(2,1)}, u32[]{:S(2)}, u32[]{:S(2)}) collective-permute-start(bf16[256,2048]{1,0:T(8,128)(2,1)} %add.236), channel_id=1, source_target_pairs={{1,0},{2,3},{5,4},{6,7},{9,8},{10,11},{13,12},{14,15},{17,16},{18,... | collective-permute-start | bytes 3145736 | tf_op jit(solution)/shard_map/ppermute | solution.py:188
  669.7 30.2 %collective-permute-start.12 = (bf16[128,2048]{1,0:T(8,128)(2,1)}, bf16[128,2048]{1,0:T(8,128)(2,1)S(1)}, u32[]{:S(2)}, u32[]{:S(2)}) collective-permute-start(bf16[128,2048]{1,0:T(8,128)(2,1)} %reduce-scatter.11.cloned.1.call-done), channel_id=1, source_target_pairs={{0,1},{3,2},{4,5},{7,6},{8,9},{11,10},{12,13},{15,14},{16,17},{19,... | collective-permute-start | bytes 1572872 | tf_op jit(solution)/shard_map/ppermute | solution.py:188
  703.4 31.8 %collective-permute-start.14 = (bf16[2048,384]{1,0:T(8,128)(2,1)S(1)}, bf16[2048,384]{1,0:T(8,128)(2,1)S(1)}, u32[]{:S(2)}, u32[]{:S(2)}) collective-permute-start(bf16[2048,384]{1,0:T(8,128)(2,1)S(1)} %add.224), channel_id=1, source_target_pairs={{1,2},{2,1},{5,6},{6,5},{9,10},{10,9},{13,14},{14,13},{17,18},{18,... | collective-permute-start | bytes 4718600 | tf_op jit(solution)/shard_map/ppermute | solution.py:188
  730.4 3.3 collective-permute-start.15
  733.9 33.5 %collective-permute-start.29 = (bf16[128,2048]{1,0:T(8,128)(2,1)S(1)}, bf16[128,2048]{1,0:T(8,128)(2,1)S(1)}, u32[]{:S(2)}, u32[]{:S(2)}) collective-permute-start(bf16[128,2048]{1,0:T(8,128)(2,1)S(1)} %add.237), channel_id=1, source_target_pairs={{1,0},{2,3},{5,4},{6,7},{9,8},{10,11},{13,12},{14,15},{17,16},{18,... | collective-permute-start | bytes 1572872 | tf_op jit(solution)/shard_map/ppermute | solution.py:188
  736.7 60.8 %collective-permute-start.28 = (bf16[2048,384]{1,0:T(8,128)(2,1)}, bf16[2048,384]{1,0:T(8,128)(2,1)}, u32[]{:S(2)}, u32[]{:S(2)}) collective-permute-start(bf16[2048,384]{1,0:T(8,128)(2,1)} %add.238), channel_id=1, source_target_pairs={{1,0},{2,3},{5,4},{6,7},{9,8},{10,11},{13,12},{14,15},{17,16},{18,... | collective-permute-start | bytes 4718600 | tf_op jit(solution)/shard_map/ppermute | solution.py:188
  (60 other events, 249.9 us)
Sparse Core Ops, SparseCore 0:
  9.9 57.0 all-gather.4
  68.9 36.7 all-gather.8
  108.1 37.4 all-gather.6
  147.3 54.3 all-gather.10
  249.5 71.2 reduce-scatter.6
  325.1 71.2 reduce-scatter.4
  444.6 55.5 reduce-scatter.10
  504.1 71.2 reduce-scatter.8
